TPU v7x, 32 devices: a whole 2x2x4 slice. The times are simulated.
32 devices in a mesh: screen: 2 (over x), pool: 8 (over z, y), dap: 2 (over core).
Axes of the slice: x: 2, y: 2, z: 4, core: 2. Of those that a mesh axis runs over, the one named last changes fastest.
Arguments:
- pair_rep: bfloat16 [352, 16, 16, 128], P(('screen', 'pool'), 'dap'), parts along dimension 0, may hold values from -6 to 6
- alignment: bfloat16 [352, 16, 16, 256], P(('screen', 'pool'), None, 'dap'), parts along dimension 0, may hold values from -6 to 6
- lengths: int32 [352], P('screen'), parts along dimension 0, may hold values from 8 to 16, as said below
- chain_breaks: int32 [352], P('screen'), parts along dimension 0, may hold values from 1 to 15, as said below
- shifts: int32 [44], P('screen'), parts along dimension 0, may hold values from 0 to 7, as said below
- alignment_proj: bfloat16 [256, 64], replicated, may hold values from -0.375 to 0.375
- outer_proj: bfloat16 [1024, 128], replicated, may hold values from -0.75 to 0.75
- chain_bias: bfloat16 [2, 128], replicated, may hold values from -4 to 4
- outgoing_ab: bfloat16 [128, 512], replicated, may hold values from -0.5 to 0.5
- outgoing_gate: bfloat16 [128, 128], replicated, may hold values from -0.5 to 0.5
- outgoing_proj: bfloat16 [128, 128], replicated, may hold values from -0.5 to 0.5
- incoming_ab: bfloat16 [128, 512], replicated, may hold values from -0.5 to 0.5
- incoming_gate: bfloat16 [128, 128], replicated, may hold values from -0.5 to 0.5
- incoming_proj: bfloat16 [128, 128], replicated, may hold values from -0.5 to 0.5
Outputs:
- pair_out: bfloat16 [352, 16, 16, 128], P(('screen', 'pool'), 'dap'), parts along dimension 0
There are 2 independent parts, one for each index of `screen`. A program takes and returns all parts, laid end to end along the dimension named above; an argument that names none is the same for every part. Nothing has to cross between parts.
Inputs may be any that keep to these rules, and one draw needn't show every extreme that they name: The complex in slot s of group g goes to group (g + shifts[s]) mod 8 and keeps slot s. No value occurs more than 6 times in shifts, and one value occurs exactly 6 times. `lengths`: at least one complex has exactly 16 residues. The bait chain is residues 0 to chain_breaks - 1, the candidate chain the rest up to the complex's length.
All inputs are finite; a program needn't handle non-finite values.
Results may differ from a plain program's by a relative error of at most 0.0066.
Values may be sent and summed in bfloat16 or wider, within the bound.
No kernel may reach another device: no remote copies, remote signals or barrier semaphores. Data moves between devices by JAX's collectives and lax.ppermute only.
A program may use at most 128 MiB of HBM per device.

v0:
```python
import functools
import itertools

import jax
import jax.numpy as jnp
import numpy as np
from jax import lax
from jax.experimental import pallas as pl
from jax.experimental.pallas import tpu as pltpu
from jax.sharding import PartitionSpec as P

EPSILON = 1e-05
F32 = jnp.float32
BF16 = jnp.bfloat16
LANES = 128
AT_ONCE = 3
VMEM_LIMIT = 24 * 2**20
PROJECT_LIMIT = 64500000
WAYS = 4
PROJECT_WAYS = 3
OUTER_AFTER = 2
BLOCK = 4
OUTER_TILES = 4


def dot(left, right):
    return jnp.dot(left, right, preferred_element_type=F32)


def normalize_steps(values, scale, ones):
    width = values.shape[-1]
    values = values - jnp.sum(values, axis=-1, keepdims=True) * (1.0 / width)
    yield
    spread = dot((values * values).astype(BF16), ones[...])
    yield
    return (values * (lax.rsqrt(spread + width * EPSILON) * scale)).astype(BF16)


def interleave(streams):
    running = list(streams)
    while running:
        for stream in list(running):
            if next(stream, running) is running:
                running.remove(stream)


def lane_groups(inner):
    group = lax.broadcasted_iota(jnp.int32, (1, LANES), 1) // inner
    return [group == q for q in range(LANES // inner)]


def project_kernel(
    place_ref,
    lengths_in,
    alignment_in,
    w_align_in,
    w_spread_in,
    own_ref,
    send_ref,
    lengths_ref,
    alignment,
    w_align,
    w_spread,
    side,
    rights,
    sems,
):
    slots, depth, rows, width = alignment.shape
    count = slots // 2
    inner = rights.shape[-1] // depth
    pieces = LANES // inner
    half, theirs, mine, home = place_ref[0], place_ref[1], place_ref[2], place_ref[3]
    copies = [
        pltpu.make_async_copy(source, target, sems.at[n])
        for n, (source, target) in enumerate(
            ((w_align_in, w_align), (lengths_in, lengths_ref), (alignment_in, alignment), (w_spread_in, w_spread))
        )
    ]
    for copy in copies:
        copy.start()
    groups = lane_groups(inner)
    source = lax.broadcasted_iota(jnp.int32, (2 * inner, 2 * LANES), 0)
    target = lax.broadcasted_iota(jnp.int32, (2 * inner, 2 * LANES), 1)
    repeat = (source == (target // LANES) * inner + target % inner).astype(BF16)
    copies[0].wait()
    w_project = lax.dot_general(
        w_align[...], repeat, (((0,), (0,)), ((), ())), preferred_element_type=F32
    ).astype(BF16)
    residue = lax.broadcasted_iota(jnp.int32, (rows, 1), 0) + half * rows
    copies[1].wait()
    copies[2].wait()

    def one(index, start, which, way, out_ref):
        length = lengths_ref[home + start + index]
        values = alignment[start + index].astype(F32).reshape(depth * rows, width)
        values = values - jnp.sum(values, axis=-1, keepdims=True) * (1.0 / width)
        yield
        spread = jnp.sum(values * values, axis=-1, keepdims=True) * (1.0 / width)
        yield
        values = dot((values * lax.rsqrt(spread + EPSILON)).astype(BF16), w_project)
        yield
        values = values.reshape(depth, rows, 2 * LANES) * jnp.where(residue < length, 1.0, 0.0)
        side[way] = values[:, :, :LANES].reshape(depth * rows, LANES) * (1.0 / depth)
        tiles = []
        for tile in range(rows // pieces):
            piece = side[way, pl.ds(tile * pieces, depth, stride=rows), :]
            for q in range(1, pieces):
                other = side[way, pl.ds(tile * pieces + q, depth, stride=rows), :]
                piece = jnp.where(groups[q], other, piece)
            tiles.append(piece)
        out_ref[index, :depth] = jnp.concatenate(tiles, axis=1).astype(BF16)
        for tile in range(depth // pieces):
            piece = values[tile * pieces, :, LANES:]
            for q in range(1, pieces):
                piece = jnp.where(groups[q], values[tile * pieces + q, :, LANES:], piece)
            rights[which, index, :, LANES * tile : LANES * tile + LANES] = piece

    ways = side.shape[0] // 2

    def step(round_, carry):
        streams = []
        for way in range(ways):
            index = jnp.minimum(round_ * ways + way, count - 1)
            streams.append(one(index, mine, 0, 2 * way, own_ref))
            streams.append(one(index, theirs, 1, 2 * way + 1, send_ref))
        interleave(streams)
        return carry

    lax.fori_loop(0, (count + ways - 1) // ways, step, 0)
    copies[3].wait()
    flat = rights[...].reshape(slots * rows, depth * inner).astype(BF16)
    spread = dot(flat, w_spread[...]).reshape(2, count, rows, depth * inner).astype(BF16)
    parts = own_ref.shape[-1]
    for which, out_ref in enumerate((own_ref, send_ref)):
        for part in range(depth * inner // parts):
            out_ref[:, depth + part * rows : depth + part * rows + rows] = spread[
                which, :, :, part * parts : part * parts + parts
            ]


def project(place, lengths, alignment, w_align, w_spread):
    slots, depth, rows, _ = alignment.shape
    count = slots // 2
    inner = w_align.shape[0] // 2
    smem = pl.BlockSpec(memory_space=pltpu.SMEM)
    vmem = pl.BlockSpec(memory_space=pltpu.VMEM)
    hbm = pl.BlockSpec(memory_space=pltpu.HBM)
    out_shape = (count, 2 * depth, rows * inner)
    return pl.pallas_call(
        project_kernel,
        out_shape=(pltpu.VMEM(out_shape, BF16), jax.ShapeDtypeStruct(out_shape, BF16)),
        in_specs=[smem, hbm, hbm, hbm, hbm],
        out_specs=(vmem, vmem),
        scratch_shapes=[
            pltpu.SMEM(lengths.shape, jnp.int32),
            pltpu.VMEM(alignment.shape, BF16),
            pltpu.VMEM(w_align.shape, BF16),
            pltpu.VMEM(w_spread.shape, BF16),
            pltpu.VMEM((2 * PROJECT_WAYS, depth * rows, LANES), F32),
            pltpu.VMEM((2, count, rows, depth * inner), F32),
            pltpu.SemaphoreType.DMA((4,)),
        ],
        compiler_params=pltpu.CompilerParams(vmem_limit_bytes=PROJECT_LIMIT),
        cost_estimate=pl.CostEstimate(flops=2 * 10**9, bytes_accessed=4 * 10**6, transcendentals=0),
        name="project",
    )(place, lengths, alignment, w_align, w_spread)


def update_kernel(
    place_ref,
    lengths_ref,
    breaks_ref,
    own_sides,
    other_sides,
    pair,
    other_pair,
    w_outer,
    bias,
    out_ab,
    out_gate,
    out_proj,
    in_ab,
    in_gate,
    in_proj,
    keep_ref,
    send_ref,
    ones,
    updates_refs,
    stream_refs,
    gates_refs,
    sides_refs,
):
    count, rows, full, width = keep_ref.shape
    depth = own_sides.shape[1] // 2
    inner = own_sides.shape[2] // rows
    pieces = LANES // inner
    sets = inner // pieces
    hidden = out_proj.shape[0]
    half = place_ref[0]
    start = place_ref[2]
    home = place_ref[3] + start
    low_is_own = half == 0
    groups = lane_groups(inner)
    zero = jnp.zeros((), BF16)
    place_j = lax.broadcasted_iota(jnp.int32, (full, 1), 0)
    ones[...] = jnp.ones_like(ones)
    unit = 0.5 * width**0.5
    pairs = full * full
    ways = updates_refs.shape[0]
    within, across = bias[0:1].astype(F32), bias[1:2].astype(F32)

    def clamp(index):
        return jnp.minimum(index, count - 1)

    def outer_update(way, step):
        own, other = own_sides[step], other_sides[step]
        low = jnp.where(low_is_own, own, other)
        high = jnp.where(low_is_own, other, own)
        right = jnp.concatenate(
            [
                jnp.concatenate(
                    [side[depth + rows * part : depth + rows * part + rows] for part in range(depth // rows)],
                    axis=1,
                )
                for side in (low, high)
            ],
            axis=0,
        )
        per = LANES // (pieces * depth)
        tiles = []
        for c2 in range(sets):
            tile = right[:, c2 // per * LANES : c2 // per * LANES + LANES]
            turn = c2 % per * pieces * depth
            tiles.append(pltpu.roll(tile, LANES - turn, 1) if turn else tile)
        right = jnp.concatenate(tiles, axis=0)
        yield
        tail = jnp.zeros((LANES - pieces * depth, 2 * LANES), BF16)
        lefts = rows // pieces
        parts = []
        for tile in range(full // pieces):
            source = low if tile < lefts else high
            at = tile % lefts * LANES
            left = source[:depth, at : at + LANES]
            turned = [left] + [pltpu.roll(left, inner * turn, 1) for turn in range(1, pieces)]
            for first_p in range(0, pieces, 2):
                column = [
                    jnp.concatenate(
                        [jnp.where(groups[q], turned[(q - p) % pieces], zero) for q in range(pieces)], axis=0
                    )
                    for p in (first_p, first_p + 1)
                ]
                stacked = jnp.concatenate([jnp.concatenate(column, axis=1), tail], axis=0)
                product = dot(right, stacked).astype(BF16)
                for k in range(2):
                    parts.append(
                        jnp.concatenate(
                            [
                                product[full * g : full * g + full, LANES * k : LANES * k + LANES]
                                for g in range(sets)
                            ],
                            axis=1,
                        )
                    )
                yield
            if (tile + 1) % OUTER_TILES == 0:
                span = len(parts) * full
                start_row = (tile + 1) * pieces * full - span
                updates_refs[way, start_row : start_row + span] = dot(
                    jnp.concatenate(parts, axis=0), w_outer[...]
                )
                parts = []
                yield

    def row_masks(length):
        column = jnp.where(place_j < length, 1.0, 0.0)
        return jnp.concatenate([jnp.where(i < length, column, 0.0) for i in range(full)], axis=0)

    def sides(values, inside, w_ab, w_gate, way, first):
        x = yield from normalize_steps(values, inside * unit, ones)
        yield
        for n in range(2):
            projected = dot(x, w_ab[:, 2 * hidden * n : 2 * hidden * n + 2 * hidden])
            sides_refs[way, first + n] = (jnp.tanh(projected[:, hidden:]) + 1.0) * projected[:, :hidden]
            yield
        gates_refs[way] = jnp.tanh(dot(x, w_gate[...])) + 1.0

    def contract(row_of, column_of):
        parts = []
        for first in range(0, full, BLOCK):
            totals = [None] * BLOCK
            for k in range(full):
                column = column_of(k)
                for i in range(BLOCK):
                    term = row_of(first + i, k) * column
                    totals[i] = term if totals[i] is None else totals[i] + term
            parts += totals
            yield
        return jnp.concatenate(parts, axis=0)

    def begin(step, way):
        stop = breaks_ref[home + step]
        head = place_j < stop
        terms = (jnp.where(head, within, across), jnp.where(head, across, within))
        chain = jnp.concatenate([jnp.where(i < stop, terms[0], terms[1]) for i in range(full)], axis=0)
        own, other = pair[start + step], other_pair[start + step]
        block = jnp.concatenate(
            [jnp.where(low_is_own, own, other), jnp.where(low_is_own, other, own)], axis=0
        )
        z1 = block.reshape(pairs, width).astype(F32) + updates_refs[way] + chain
        stream_refs[way] = z1
        yield
        yield from sides(z1, row_masks(lengths_ref[home + step]), out_ab, out_gate, way, 0)

    def middle(step, way):
        t = yield from contract(
            lambda i, k: sides_refs[way, 0, pl.ds(full * i + k, 1), :],
            lambda k: sides_refs[way, 1, pl.ds(k, full, stride=full), :],
        )
        u = yield from normalize_steps(t, unit, ones)
        yield
        z2 = stream_refs[way] + gates_refs[way] * dot(u, out_proj[...])
        z2 = z2.astype(BF16).astype(F32)
        stream_refs[way] = z2
        yield
        yield from sides(z2, row_masks(lengths_ref[home + step]), in_ab, in_gate, way, 2)

    def last(step, way):
        t = yield from contract(
            lambda i, k: sides_refs[way, 3, pl.ds(full * k + i, 1), :],
            lambda k: sides_refs[way, 2, full * k : full * k + full],
        )
        u = yield from normalize_steps(t, unit, ones)
        yield
        y3 = stream_refs[way] + gates_refs[way] * dot(u, in_proj[...])
        y3 = (y3 * row_masks(lengths_ref[home + step])).astype(BF16)
        low = y3[: rows * full].reshape(rows, full, width)
        high = y3[rows * full :].reshape(rows, full, width)
        keep_ref[step] = jnp.where(low_is_own, low, high)
        send_ref[step] = jnp.where(low_is_own, high, low)

    def whole(step, way):
        yield from begin(step, way)
        yield
        yield from middle(step, way)
        yield
        yield from last(step, way)

    def later(streams, ticks):
        for _ in range(ticks):
            yield
        for stream in streams:
            yield from stream

    def round_of(steps, ahead):
        streams = [whole(step, way) for way, step in enumerate(steps)]
        outers = [outer_update(way, step) for way, step in enumerate(ahead)]
        interleave(streams + [later(outers, OUTER_AFTER)])

    def both(round_, carry):
        base = round_ * ways
        round_of([base + way for way in range(ways)], [clamp(base + ways + way) for way in range(ways)])
        return carry

    rounds = (count + ways - 1) // ways
    interleave([outer_update(way, clamp(way)) for way in range(ways)])
    lax.fori_loop(0, rounds - 1, both, 0)
    round_of(list(range((rounds - 1) * ways, count)), [])


def update(place, lengths, breaks, own_sides, other_sides, pair, other_pair, weights):
    outer_proj, chain_bias, out_ab, out_gate, out_proj, in_ab, in_gate, in_proj = weights
    count = own_sides.shape[0]
    _, full, width = pair.shape[1:]
    smem = pl.BlockSpec(memory_space=pltpu.SMEM)
    vmem = pl.BlockSpec(memory_space=pltpu.VMEM)
    shape = jax.ShapeDtypeStruct((count,) + pair.shape[1:], BF16)
    pairs, hidden = full * full, out_proj.shape[0]
    return pl.pallas_call(
        update_kernel,
        out_shape=(shape, shape),
        in_specs=[smem] * 3 + [vmem] * 12,
        out_specs=(vmem, vmem),
        scratch_shapes=[
            pltpu.VMEM((width, width), BF16),
            pltpu.VMEM((WAYS, pairs, width), F32),
            pltpu.VMEM((WAYS, pairs, width), F32),
            pltpu.VMEM((WAYS, pairs, width), F32),
            pltpu.VMEM((WAYS, 4, pairs, hidden), F32),
        ],
        compiler_params=pltpu.CompilerParams(vmem_limit_bytes=VMEM_LIMIT),
        cost_estimate=pl.CostEstimate(flops=10**10, bytes_accessed=4 * 10**6, transcendentals=0),
        name="pair_update",
    )(
        place,
        lengths,
        breaks,
        own_sides,
        other_sides,
        pair,
        other_pair,
        outer_proj,
        chain_bias,
        out_ab,
        out_gate,
        out_proj,
        in_ab,
        in_gate,
        in_proj,
    )


def spread_matrix(depth, inner):
    pieces = LANES // inner
    r, c2 = np.divmod(np.arange(depth * inner), inner)
    matrix = np.zeros((depth * inner, depth * inner), np.float32)
    matrix[np.arange(depth * inner), (c2 // pieces) * pieces * depth + (c2 % pieces) * depth + r] = 1.0
    return jnp.asarray(matrix, BF16)


def build_tables(shifts_ref, table, counts, capacity):
    slots, groups = shifts_ref.shape[0], counts.shape[0]
    for v in range(groups):
        counts[v] = 0

    def step(slot, carry):
        v = shifts_ref[slot]
        rank = counts[v]
        table[v * capacity + rank] = slot
        counts[v] = rank + 1
        return carry

    lax.fori_loop(0, slots, step, 0)


def list_large(counts, large, low):
    for k in range(large.shape[0]):
        large[k] = 0
    found = jnp.int32(0)
    for v in range(1, counts.shape[0]):
        many = counts[v] > low

        @pl.when(many)
        def _(found=found, v=v):
            large[found] = v

        found = found + many.astype(jnp.int32)
    return found


def subsets(groups, most):
    return [c for n in range(most + 1) for c in itertools.combinations(range(1, groups), n)]


def pack_kernel(low, capacity, half_ref, shifts_ref, keep, other, *refs):
    branch, table, counts, large = refs[-4:]
    groups = counts.shape[0]
    outs = refs[:-4]
    statics, rests = outs[: groups - 1], outs[groups - 1 :]
    count = keep.shape[0]
    base = half_ref[0] * count
    build_tables(shifts_ref, table, counts, capacity)
    found = list_large(counts, large, low)
    taken = [large[k] for k in range(min(AT_ONCE, large.shape[0]))]
    index = jnp.int32(0)
    for n, subset in enumerate(subsets(groups, AT_ONCE)):
        same = functools.reduce(
            jnp.logical_and, [t == (subset[k] if k < len(subset) else 0) for k, t in enumerate(taken)]
        )
        index = jnp.where(same, n, index)
    branch[0] = index
    branch[1] = found
    for k in range(AT_ONCE, large.shape[0]):
        branch[2 + k - AT_ONCE] = large[k]

    def fetch(v, rank):
        slot = jnp.where(rank < counts[v], table[v * capacity + rank], 0)
        at = slot - base
        mine = (at >= 0) & (at < count)
        near = keep[jnp.clip(at, 0, count - 1)]
        far = other[jnp.clip(slot - (count - base), 0, count - 1)]
        return jnp.where(mine, near, far)

    for v in range(1, groups):
        for rank in range(low):
            statics[v - 1][rank] = fetch(v, rank)
    for k, rest in enumerate(rests):
        @pl.when(k < found)
        def _(k=k, rest=rest):
            v = large[k]
            for rank in range(low, capacity):
                rest[rank - low] = fetch(v, rank)


def unpack_kernel(low, capacity, half_ref, shifts_ref, keep, other, *refs):
    out, table, counts, large, sem = refs[-5:]
    groups = counts.shape[0]
    statics, rests = refs[: groups - 1], refs[groups - 1 : -5]
    count = keep.shape[0]
    base = half_ref[0] * count
    build_tables(shifts_ref, table, counts, capacity)
    found = list_large(counts, large, low)

    def put(source, slot):
        pltpu.make_async_copy(source, out.at[slot], sem).start()

    for v in range(1, groups):
        for rank in range(low):

            @pl.when(rank < counts[v])
            def _(v=v, rank=rank):
                put(statics[v - 1].at[rank], table[v * capacity + rank])

    def step(rank, carry):
        slot = table[rank]
        at = slot - base
        mine = (at >= 0) & (at < count)

        @pl.when(mine)
        def _():
            put(keep.at[jnp.clip(at, 0, count - 1)], slot)

        @pl.when(jnp.logical_not(mine))
        def _():
            put(other.at[jnp.clip(slot - (count - base), 0, count - 1)], slot)

        return carry

    lax.fori_loop(0, counts[0], step, 0)
    for k, rest in enumerate(rests):
        for rank in range(low, capacity):

            @pl.when((k < found) & (rank < counts[large[k]]))
            def _(k=k, rank=rank, rest=rest):
                put(rest.at[rank - low], table[large[k] * capacity + rank])

    pltpu.make_async_copy(out, out, sem).wait()


def exchange(half, shifts, keep, other, group_count, capacity):
    slots = shifts.shape[0]
    low = capacity // 2
    most = min(slots // (low + 1), group_count - 1)
    most = max(most, AT_ONCE)
    block = keep.shape[1:]
    smem = pl.BlockSpec(memory_space=pltpu.SMEM)
    vmem = pl.BlockSpec(memory_space=pltpu.VMEM)
    anywhere = pl.BlockSpec(memory_space=pl.ANY)
    tables = [
        pltpu.SMEM((group_count * capacity,), jnp.int32),
        pltpu.SMEM((group_count,), jnp.int32),
        pltpu.SMEM((most,), jnp.int32),
        pltpu.SemaphoreType.DMA,
    ]
    params = pltpu.CompilerParams(vmem_limit_bytes=VMEM_LIMIT)
    low_shape = jax.ShapeDtypeStruct((low,) + block, BF16)
    high_shape = jax.ShapeDtypeStruct((capacity - low,) + block, BF16)
    packed = pl.pallas_call(
        functools.partial(pack_kernel, low, capacity),
        out_shape=[low_shape] * (group_count - 1)
        + [high_shape] * most
        + [jax.ShapeDtypeStruct((2 + most - AT_ONCE,), jnp.int32)],
        in_specs=[smem, smem, vmem, vmem],
        out_specs=[vmem] * (group_count - 1 + most) + [smem],
        scratch_shapes=tables[:-1],
        compiler_params=params,
        name="pack",
    )(half, shifts, keep, other)
    statics = packed[: group_count - 1]
    rests = packed[group_count - 1 : -1]
    branch = packed[-1]

    def move(block, v):
        return lax.ppermute(block, "pool", [(g, (g + v) % group_count) for g in range(group_count)])

    arrived = {}
    for v in range(1, group_count):
        arrived[v] = move(statics[v - 1], v)
    arrived = [arrived[v] for v in range(1, group_count)]

    def choice(subset):
        def run(*blocks):
            moved = [move(block, v) for block, v in zip(blocks, subset)]
            return tuple(moved) + blocks[len(subset) :]

        return run

    late = list(
        lax.switch(
            branch[0], [choice(subset) for subset in subsets(group_count, AT_ONCE)], *rests[:AT_ONCE]
        )
    )
    if most > AT_ONCE:

        def more(*blocks):
            singles = [choice(subset) for subset in subsets(group_count, 1)]
            return tuple(lax.switch(branch[2 + k], singles, block)[0] for k, block in enumerate(blocks))

        late += lax.cond(branch[1] > AT_ONCE, more, lambda *blocks: blocks, *rests[AT_ONCE:])
    return pl.pallas_call(
        functools.partial(unpack_kernel, low, capacity),
        out_shape=jax.ShapeDtypeStruct((slots,) + block, BF16),
        in_specs=[smem, smem] + [vmem] * (2 + group_count - 1 + most),
        out_specs=anywhere,
        scratch_shapes=tables,
        compiler_params=params,
        name="unpack",
    )(half, shifts, keep, other, *arrived, *late)


def exchange_padded(half, shifts, keep, other, group_count, capacity):
    slots = shifts.shape[0]
    my_group = lax.axis_index("pool")
    blocks = jnp.where(
        half == 0, jnp.concatenate([keep, other], axis=0), jnp.concatenate([other, keep], axis=0)
    )
    slot = jnp.arange(slots, dtype=jnp.int32)
    earlier = (shifts[None, :] == shifts[:, None]) & (slot[None, :] < slot[:, None])
    rank = jnp.sum(earlier.astype(jnp.int32), axis=1)
    send_at = (my_group + shifts) % group_count * capacity + rank
    receive_at = (my_group - shifts) % group_count * capacity + rank
    place = jnp.arange(group_count * capacity, dtype=jnp.int32)
    source = jnp.sum(jnp.where(send_at[None, :] == place[:, None], slot[None, :], 0), axis=1)
    received = lax.all_to_all(
        jnp.take(blocks, source, axis=0), "pool", split_axis=0, concat_axis=0, tiled=True
    )
    return jnp.take(received, receive_at, axis=0)


def body(pair_rep, alignment, lengths, chain_breaks, shifts, *weights):
    group_count = lax.axis_size("pool")
    slot_count = pair_rep.shape[0]
    count = slot_count // 2
    capacity = max(2, (2 * slot_count + group_count - 1) // group_count)
    half = lax.axis_index("dap").astype(jnp.int32)
    swap = [(0, 1), (1, 0)]
    place = jnp.stack([half, (1 - half) * count, half * count, lax.axis_index("pool") * slot_count])
    place = place.astype(jnp.int32)
    alignment_proj, outer_proj = weights[:2]
    inner = alignment_proj.shape[1] // 2
    w_spread = spread_matrix(alignment.shape[1], inner)
    w_outer = (
        outer_proj.reshape(inner, inner, -1).transpose(1, 0, 2).reshape(outer_proj.shape)
    )
    other_pair = lax.ppermute(pair_rep, "dap", swap)
    own_sides, send_sides = project(place, lengths, alignment, alignment_proj.T, w_spread)
    other_sides = lax.ppermute(send_sides, "dap", swap)
    keep, send = update(
        place, lengths, chain_breaks, own_sides, other_sides, pair_rep, other_pair, (w_outer,) + weights[2:]
    )
    other = lax.ppermute(send, "dap", swap)
    move = exchange if group_count <= 8 else exchange_padded
    return move(half.reshape(1), shifts, keep, other, group_count, capacity)


def solution(mesh):
    step = sharded(mesh)
    return step


def sharded(mesh):
    return jax.shard_map(
        body,
        mesh=mesh,
        in_specs=(
            P(("screen", "pool"), "dap", None, None),
            P(("screen", "pool"), None, "dap", None),
            P("screen"),
            P("screen"),
            P("screen"),
        )
        + (P(),) * 9,
        out_specs=P(("screen", "pool"), "dap", None, None),
        check_vma=False,
    )
```

profile of v0, /device:TPU:15, one launch (start us, length us, event | category | flops | bytes accessed | tf_op | source)
XLA Modules:
  0.0 63.0 jit_solution(6295062592185978828)
XLA Ops:
  0.0 0.7 %collective-permute-start.169 = (bf16[22,8,16,128]{3,2,1,0:T(8,128)(2,1)}, bf16[22,8,16,128]{3,2,1,0:T(8,128)(2,1)S(1)}, u32[]{:S(2)}, u32[]{:S(2)}) collective-permute-start(bf16[22,8,16,128]{3,2,1,0:T(8,128)(2,1)} %pair.1), channel_id=1, source_target_pairs={{0,1},{1,0},{2,3},{3,2},{4,5},{5,4},{6,7},{7,6},{8,9},{9,8},{10,11... | collective-permute-start | bytes 2162696 | tf_op jit(solution)/shard_map/ppermute | solution.py:644
  0.7 0.6 pad_add_fusion.place_ref
  1.4 5.1 %project.1 = (bf16[11,32,256]{2,1,0:T(8,128)(2,1)S(1)}, bf16[11,32,256]{2,1,0:T(8,128)(2,1)}) custom-call(s32[4]{0:T(128)} %pad_add_fusion.place_ref, s32[176]{0:T(256)} %lengths_ref.1, bf16[22,16,8,256]{3,2,1,0:T(8,128)(2,1)} %alignment_in.1, bf16[64,256]{1,0:T(8,128)(2,1)} %bitcast.15, bf16[512,512]{1,0:T(8,128)(2,1)} %constant.33.clone.w_spread_in), custom_call_target="tpu_custom_call" | custom-call | flops 2000000000 | bytes 4000000 | tf_op jit(solution)/shard_map/project/pallas_call | solution.py:149
  6.7 1.5 %collective-permute-done.168.other_sides = bf16[11,32,256]{2,1,0:T(8,128)(2,1)S(1)} collective-permute-done((bf16[11,32,256]{2,1,0:T(8,128)(2,1)}, bf16[11,32,256]{2,1,0:T(8,128)(2,1)S(1)}, u32[]{:S(2)}, u32[]{:S(2)}) %collective-permute-start.168) | collective-permute-done | bytes 180256 | tf_op jit(solution)/shard_map/ppermute | solution.py:646
  8.3 13.2 %pair_update.1 = (bf16[11,8,16,128]{3,2,1,0:T(8,128)(2,1)S(1)}, bf16[11,8,16,128]{3,2,1,0:T(8,128)(2,1)S(1)}) custom-call(s32[4]{0:T(128)S(1)} %copy-done.1, s32[176]{0:T(256)S(1)} %copy-done.9, s32[176]{0:T(256)S(1)} %copy-done.10, bf16[11,32,256]{2,1,0:T(8,128)(2,1)S(1)} %get-tuple-element.647.own_sides, ...), custom_call_target="tpu_custom_call" | custom-call | flops 10000000000 | bytes 4000000 | tf_op jit(solution)/shard_map/pair_update/pallas_call | solution.py:378
  21.6 0.2 collective-permute-start.170
  21.8 1.5 %collective-permute-done.170.other = bf16[11,8,16,128]{3,2,1,0:T(8,128)(2,1)S(1)} collective-permute-done((bf16[11,8,16,128]{3,2,1,0:T(8,128)(2,1)S(1)}, bf16[11,8,16,128]{3,2,1,0:T(8,128)(2,1)S(1)}, u32[]{:S(2)}, u32[]{:S(2)}) %collective-permute-start.170) | collective-permute-done | bytes 360480 | tf_op jit(solution)/shard_map/ppermute | solution.py:650
  23.3 1.9 %pack.1 = (bf16[3,8,16,128]{3,2,1,0:T(8,128)(2,1)S(1)}, bf16[3,8,16,128]{3,2,1,0:T(8,128)(2,1)S(1)}, bf16[3,8,16,128]{3,2,1,0:T(8,128)(2,1)S(1)}, bf16[3,8,16,12...) custom-call(s32[1]{0:T(128)} %bitcast.2.half_ref, ...), custom_call_target="tpu_custom_call" | custom-call | tf_op jit(solution)/shard_map/pack/pallas_call | solution.py:557
  25.3 1.3 %collective-permute-start.171 = (bf16[3,8,16,128]{3,2,1,0:T(8,128)(2,1)S(1)}, bf16[3,8,16,128]{3,2,1,0:T(8,128)(2,1)S(1)}, u32[]{:S(2)}, u32[]{:S(2)}) collective-permute-start(bf16[3,8,16,128]{3,2,1,0:T(8,128)(2,1)S(1)} %get-tuple-element.651), channel_id=1, source_target_pairs={{0,2},{2,4},{4,6},{6,8},{8,10},{10,12},{12,14},{14,0},{1,3},{3,5},... | collective-permute-start | bytes 294920 | tf_op jit(solution)/shard_map/ppermute | solution.py:573
  26.6 1.3 %collective-permute-start.172 = (bf16[3,8,16,128]{3,2,1,0:T(8,128)(2,1)S(1)}, bf16[3,8,16,128]{3,2,1,0:T(8,128)(2,1)S(1)}, u32[]{:S(2)}, u32[]{:S(2)}) collective-permute-start(bf16[3,8,16,128]{3,2,1,0:T(8,128)(2,1)S(1)} %get-tuple-element.652), channel_id=1, source_target_pairs={{0,4},{2,6},{4,8},{6,10},{8,12},{10,14},{12,0},{14,2},{1,5},{3,7},... | collective-permute-start | bytes 294920 | tf_op jit(solution)/shard_map/ppermute | solution.py:573
  27.9 0.6 fusion.1
  29.7 13.3 %conditional.4 = ((bf16[3,8,16,128]{3,2,1,0:T(8,128)(2,1)S(1)}, bf16[3,8,16,128]{3,2,1,0:T(8,128)(2,1)S(1)}, bf16[3,8,16,128]{3,2,1,0:T(8,128)(2,1)S(1)})) conditional(s32[]{:T(128)} %bitcast.10, (bf16[3,8,16,128]{3,2,1,0:T(8,128)(2,1)S(1)}, bf16[3,8,16,128]{3,2,1,0:T(8,128)(2,1)S(1)}, ...), branch_computations={%region_0.0_spmd, %region_1.0_spmd, %region_2.0_spmd, %region_3.0_... | conditional | bytes 1769624 | solution.py:588
  30.0 1.0 %collective-permute-start.127 = (bf16[3,8,16,128]{3,2,1,0:T(8,128)(2,1)S(1)}, bf16[3,8,16,128]{3,2,1,0:T(8,128)(2,1)S(1)}, u32[]{:S(2)}, u32[]{:S(2)}) collective-permute-start(bf16[3,8,16,128]{3,2,1,0:T(8,128)(2,1)S(1)} %get-tuple-element.595), channel_id=1, source_target_pairs={{0,6},{2,8},{4,10},{6,12},{8,14},{10,0},{12,2},{14,4},{1,7},{3,9},... | collective-permute-start | bytes 294920 | tf_op jit(solution)/shard_map/cond/branch_55_fun/ppermute | solution.py:573
  31.0 1.3 %collective-permute-start.128 = (bf16[3,8,16,128]{3,2,1,0:T(8,128)(2,1)S(1)}, bf16[3,8,16,128]{3,2,1,0:T(8,128)(2,1)S(1)}, u32[]{:S(2)}, u32[]{:S(2)}) collective-permute-start(bf16[3,8,16,128]{3,2,1,0:T(8,128)(2,1)S(1)} %get-tuple-element.596), channel_id=1, source_target_pairs={{0,8},{2,10},{4,12},{6,14},{8,0},{10,2},{12,4},{14,6},{1,9},{3,11}... | collective-permute-start | bytes 294920 | tf_op jit(solution)/shard_map/cond/branch_55_fun/ppermute | solution.py:573
  32.5 1.9 %collective-permute-done.127 = bf16[3,8,16,128]{3,2,1,0:T(8,128)(2,1)S(1)} collective-permute-done((bf16[3,8,16,128]{3,2,1,0:T(8,128)(2,1)S(1)}, bf16[3,8,16,128]{3,2,1,0:T(8,128)(2,1)S(1)}, u32[]{:S(2)}, u32[]{:S(2)}) %collective-permute-start.127) | collective-permute-done | bytes 98336 | tf_op jit(solution)/shard_map/cond/branch_55_fun/ppermute | solution.py:573
  34.5 6.8 %collective-permute-done.128 = bf16[3,8,16,128]{3,2,1,0:T(8,128)(2,1)S(1)} collective-permute-done((bf16[3,8,16,128]{3,2,1,0:T(8,128)(2,1)S(1)}, bf16[3,8,16,128]{3,2,1,0:T(8,128)(2,1)S(1)}, u32[]{:S(2)}, u32[]{:S(2)}) %collective-permute-start.128) | collective-permute-done | bytes 98336 | tf_op jit(solution)/shard_map/cond/branch_55_fun/ppermute | solution.py:573
  41.3 1.7 %collective-permute-done.129 = bf16[3,8,16,128]{3,2,1,0:T(8,128)(2,1)S(1)} collective-permute-done((bf16[3,8,16,128]{3,2,1,0:T(8,128)(2,1)S(1)}, bf16[3,8,16,128]{3,2,1,0:T(8,128)(2,1)S(1)}, u32[]{:S(2)}, u32[]{:S(2)}) %collective-permute-start.129) | collective-permute-done | bytes 98336 | tf_op jit(solution)/shard_map/cond/branch_55_fun/ppermute | solution.py:573
  43.1 2.2 %collective-permute-start.174 = (bf16[3,8,16,128]{3,2,1,0:T(8,128)(2,1)S(1)}, bf16[3,8,16,128]{3,2,1,0:T(8,128)(2,1)S(1)}, u32[]{:S(2)}, u32[]{:S(2)}) collective-permute-start(bf16[3,8,16,128]{3,2,1,0:T(8,128)(2,1)S(1)} %get-tuple-element.654), channel_id=1, source_target_pairs={{0,8},{2,10},{4,12},{6,14},{8,0},{10,2},{12,4},{14,6},{1,9},{3,11}... | collective-permute-start | bytes 294920 | tf_op jit(solution)/shard_map/ppermute | solution.py:573
  45.2 1.6 %collective-permute-start.175 = (bf16[3,8,16,128]{3,2,1,0:T(8,128)(2,1)S(1)}, bf16[3,8,16,128]{3,2,1,0:T(8,128)(2,1)S(1)}, u32[]{:S(2)}, u32[]{:S(2)}) collective-permute-start(bf16[3,8,16,128]{3,2,1,0:T(8,128)(2,1)S(1)} %get-tuple-element.655), channel_id=1, source_target_pairs={{0,10},{2,12},{4,14},{6,0},{8,2},{10,4},{12,6},{14,8},{1,11},{3,13... | collective-permute-start | bytes 294920 | tf_op jit(solution)/shard_map/ppermute | solution.py:573
  46.8 0.3 collective-permute-start.177
  47.1 6.9 %collective-permute-done.173.refs_2_ = bf16[3,8,16,128]{3,2,1,0:T(8,128)(2,1)S(1)} collective-permute-done((bf16[3,8,16,128]{3,2,1,0:T(8,128)(2,1)S(1)}, bf16[3,8,16,128]{3,2,1,0:T(8,128)(2,1)S(1)}, u32[]{:S(2)}, u32[]{:S(2)}) %collective-permute-start.173) | collective-permute-done | bytes 98336 | tf_op jit(solution)/shard_map/ppermute | solution.py:573
  54.0 2.1 %collective-permute-done.174.refs_3_ = bf16[3,8,16,128]{3,2,1,0:T(8,128)(2,1)S(1)} collective-permute-done((bf16[3,8,16,128]{3,2,1,0:T(8,128)(2,1)S(1)}, bf16[3,8,16,128]{3,2,1,0:T(8,128)(2,1)S(1)}, u32[]{:S(2)}, u32[]{:S(2)}) %collective-permute-start.174) | collective-permute-done | bytes 98336 | tf_op jit(solution)/shard_map/ppermute | solution.py:573
  56.3 4.9 %collective-permute-done.177.refs_6_ = bf16[3,8,16,128]{3,2,1,0:T(8,128)(2,1)S(1)} collective-permute-done((bf16[3,8,16,128]{3,2,1,0:T(8,128)(2,1)S(1)}, bf16[3,8,16,128]{3,2,1,0:T(8,128)(2,1)S(1)}, u32[]{:S(2)}, u32[]{:S(2)}) %collective-permute-start.177) | collective-permute-done | bytes 98336 | tf_op jit(solution)/shard_map/ppermute | solution.py:573
  61.1 1.7 %unpack.1 = bf16[22,8,16,128]{3,2,1,0:T(8,128)(2,1)} custom-call(s32[1]{0:T(128)} %bitcast.2.half_ref, s32[22]{0:T(128)S(1)} %copy-done, bf16[11,8,16,128]{3,2,1,0:T(8,128)(2,1)S(1)} %get-tuple-element.649.keep, bf16[11,8,16,128]{3,2,1,0:T(8,128)(2,1)S(1)} %collective-permute-done.170.other, bf16[3,8,16,128]{3,2,1,0:T(8,128)(2,1)S(1)} %collective-permute-done.171.refs_0_, ...), custom_call_target="tpu_custom_call" | custom-call | tf_op jit(solution)/shard_map/unpack/pallas_call | solution.py:599
  (40 shorter events, 0.7 us)
Async XLA Ops:
  0.0 8.2 %collective-permute-start.169 = (bf16[22,8,16,128]{3,2,1,0:T(8,128)(2,1)}, bf16[22,8,16,128]{3,2,1,0:T(8,128)(2,1)S(1)}, u32[]{:S(2)}, u32[]{:S(2)}) collective-permute-start(bf16[22,8,16,128]{3,2,1,0:T(8,128)(2,1)} %pair.1), channel_id=1, source_target_pairs={{0,1},{1,0},{2,3},{3,2},{4,5},{5,4},{6,7},{7,6},{8,9},{9,8},{10,11... | collective-permute-start | bytes 2162696 | tf_op jit(solution)/shard_map/ppermute | solution.py:644
  1.3 6.9 %copy-start.1 = (s32[4]{0:T(128)S(1)}, s32[4]{0:T(128)}, u32[]{:S(2)}) copy-start(s32[4]{0:T(128)} %pad_add_fusion.place_ref) | copy-start | bytes 52
  1.3 6.9 %copy-start.2 = (bf16[22,8,16,128]{3,2,1,0:T(8,128)(2,1)S(1)}, bf16[22,8,16,128]{3,2,1,0:T(8,128)(2,1)}, u32[]{:S(2)}) copy-start(bf16[22,8,16,128]{3,2,1,0:T(8,128)(2,1)} %pair.1) | copy-start | bytes 2162692
  1.3 7.0 %copy-start.3 = (bf16[128,512]{1,0:T(8,128)(2,1)S(1)}, bf16[128,512]{1,0:T(8,128)(2,1)}, u32[]{:S(2)}) copy-start(bf16[128,512]{1,0:T(8,128)(2,1)} %out_ab.1) | copy-start | bytes 393220
  1.3 7.0 %copy-start.4 = (bf16[128,512]{1,0:T(8,128)(2,1)S(1)}, bf16[128,512]{1,0:T(8,128)(2,1)}, u32[]{:S(2)}) copy-start(bf16[128,512]{1,0:T(8,128)(2,1)} %in_ab.1) | copy-start | bytes 393220
  1.3 7.0 %copy-start.5 = (bf16[128,128]{1,0:T(8,128)(2,1)S(1)}, bf16[128,128]{1,0:T(8,128)(2,1)}, u32[]{:S(2)}) copy-start(bf16[128,128]{1,0:T(8,128)(2,1)} %out_gate.1) | copy-start | bytes 98308
  1.3 7.0 %copy-start.6 = (bf16[128,128]{1,0:T(8,128)(2,1)S(1)}, bf16[128,128]{1,0:T(8,128)(2,1)}, u32[]{:S(2)}) copy-start(bf16[128,128]{1,0:T(8,128)(2,1)} %out_proj.1) | copy-start | bytes 98308
  1.3 7.0 %copy-start.7 = (bf16[128,128]{1,0:T(8,128)(2,1)S(1)}, bf16[128,128]{1,0:T(8,128)(2,1)}, u32[]{:S(2)}) copy-start(bf16[128,128]{1,0:T(8,128)(2,1)} %in_gate.1) | copy-start | bytes 98308
  1.3 6.9 %copy-start.8 = (bf16[128,128]{1,0:T(8,128)(2,1)S(1)}, bf16[128,128]{1,0:T(8,128)(2,1)}, u32[]{:S(2)}) copy-start(bf16[128,128]{1,0:T(8,128)(2,1)} %in_proj.1) | copy-start | bytes 98308
  1.4 6.9 %copy-start.9 = (s32[176]{0:T(256)S(1)}, s32[176]{0:T(256)}, u32[]{:S(2)}) copy-start(s32[176]{0:T(256)} %lengths_ref.1) | copy-start | bytes 2116
  1.4 6.9 %copy-start.10 = (s32[176]{0:T(256)S(1)}, s32[176]{0:T(256)}, u32[]{:S(2)}) copy-start(s32[176]{0:T(256)} %breaks_ref.1) | copy-start | bytes 2116
  6.5 1.7 %collective-permute-start.168 = (bf16[11,32,256]{2,1,0:T(8,128)(2,1)}, bf16[11,32,256]{2,1,0:T(8,128)(2,1)S(1)}, u32[]{:S(2)}, u32[]{:S(2)}) collective-permute-start(bf16[11,32,256]{2,1,0:T(8,128)(2,1)} %get-tuple-element.648), channel_id=1, source_target_pairs={{0,1},{1,0},{2,3},{3,2},{4,5},{5,4},{6,7},{7,6},{8,9},{9,8},{10,11... | collective-permute-start | bytes 540680 | tf_op jit(solution)/shard_map/ppermute | solution.py:646
  8.3 15.0 %copy-start = (s32[22]{0:T(128)S(1)}, s32[22]{0:T(128)}, u32[]{:S(2)}) copy-start(s32[22]{0:T(128)} %shifts_ref.3) | copy-start | bytes 268
  21.6 1.7 %collective-permute-start.170 = (bf16[11,8,16,128]{3,2,1,0:T(8,128)(2,1)S(1)}, bf16[11,8,16,128]{3,2,1,0:T(8,128)(2,1)S(1)}, u32[]{:S(2)}, u32[]{:S(2)}) collective-permute-start(bf16[11,8,16,128]{3,2,1,0:T(8,128)(2,1)S(1)} %get-tuple-element.650), channel_id=1, source_target_pairs={{0,1},{1,0},{2,3},{3,2},{4,5},{5,4},{6,7},{7,6},{8,9},{9,8},{10,11... | collective-permute-start | bytes 1081352 | tf_op jit(solution)/shard_map/ppermute | solution.py:650
  25.3 21.6 %collective-permute-start.171 = (bf16[3,8,16,128]{3,2,1,0:T(8,128)(2,1)S(1)}, bf16[3,8,16,128]{3,2,1,0:T(8,128)(2,1)S(1)}, u32[]{:S(2)}, u32[]{:S(2)}) collective-permute-start(bf16[3,8,16,128]{3,2,1,0:T(8,128)(2,1)S(1)} %get-tuple-element.651), channel_id=1, source_target_pairs={{0,2},{2,4},{4,6},{6,8},{8,10},{10,12},{12,14},{14,0},{1,3},{3,5},... | collective-permute-start | bytes 294920 | tf_op jit(solution)/shard_map/ppermute | solution.py:573
  26.6 20.3 %collective-permute-start.172 = (bf16[3,8,16,128]{3,2,1,0:T(8,128)(2,1)S(1)}, bf16[3,8,16,128]{3,2,1,0:T(8,128)(2,1)S(1)}, u32[]{:S(2)}, u32[]{:S(2)}) collective-permute-start(bf16[3,8,16,128]{3,2,1,0:T(8,128)(2,1)S(1)} %get-tuple-element.652), channel_id=1, source_target_pairs={{0,4},{2,6},{4,8},{6,10},{8,12},{10,14},{12,0},{14,2},{1,5},{3,7},... | collective-permute-start | bytes 294920 | tf_op jit(solution)/shard_map/ppermute | solution.py:573
  30.0 4.4 %collective-permute-start.127 = (bf16[3,8,16,128]{3,2,1,0:T(8,128)(2,1)S(1)}, bf16[3,8,16,128]{3,2,1,0:T(8,128)(2,1)S(1)}, u32[]{:S(2)}, u32[]{:S(2)}) collective-permute-start(bf16[3,8,16,128]{3,2,1,0:T(8,128)(2,1)S(1)} %get-tuple-element.595), channel_id=1, source_target_pairs={{0,6},{2,8},{4,10},{6,12},{8,14},{10,0},{12,2},{14,4},{1,7},{3,9},... | collective-permute-start | bytes 294920 | tf_op jit(solution)/shard_map/cond/branch_55_fun/ppermute | solution.py:573
  31.0 10.2 %collective-permute-start.128 = (bf16[3,8,16,128]{3,2,1,0:T(8,128)(2,1)S(1)}, bf16[3,8,16,128]{3,2,1,0:T(8,128)(2,1)S(1)}, u32[]{:S(2)}, u32[]{:S(2)}) collective-permute-start(bf16[3,8,16,128]{3,2,1,0:T(8,128)(2,1)S(1)} %get-tuple-element.596), channel_id=1, source_target_pairs={{0,8},{2,10},{4,12},{6,14},{8,0},{10,2},{12,4},{14,6},{1,9},{3,11}... | collective-permute-start | bytes 294920 | tf_op jit(solution)/shard_map/cond/branch_55_fun/ppermute | solution.py:573
  32.4 10.6 %collective-permute-start.129 = (bf16[3,8,16,128]{3,2,1,0:T(8,128)(2,1)S(1)}, bf16[3,8,16,128]{3,2,1,0:T(8,128)(2,1)S(1)}, u32[]{:S(2)}, u32[]{:S(2)}) collective-permute-start(bf16[3,8,16,128]{3,2,1,0:T(8,128)(2,1)S(1)} %get-tuple-element.597), channel_id=1, source_target_pairs={{0,12},{2,14},{4,0},{6,2},{8,4},{10,6},{12,8},{14,10},{1,13},{3,15... | collective-permute-start | bytes 294920 | tf_op jit(solution)/shard_map/cond/branch_55_fun/ppermute | solution.py:573
  43.0 11.0 %collective-permute-start.173 = (bf16[3,8,16,128]{3,2,1,0:T(8,128)(2,1)S(1)}, bf16[3,8,16,128]{3,2,1,0:T(8,128)(2,1)S(1)}, u32[]{:S(2)}, u32[]{:S(2)}) collective-permute-start(bf16[3,8,16,128]{3,2,1,0:T(8,128)(2,1)S(1)} %get-tuple-element.653), channel_id=1, source_target_pairs={{0,6},{2,8},{4,10},{6,12},{8,14},{10,0},{12,2},{14,4},{1,7},{3,9},... | collective-permute-start | bytes 294920 | tf_op jit(solution)/shard_map/ppermute | solution.py:573
  43.1 13.0 %collective-permute-start.174 = (bf16[3,8,16,128]{3,2,1,0:T(8,128)(2,1)S(1)}, bf16[3,8,16,128]{3,2,1,0:T(8,128)(2,1)S(1)}, u32[]{:S(2)}, u32[]{:S(2)}) collective-permute-start(bf16[3,8,16,128]{3,2,1,0:T(8,128)(2,1)S(1)} %get-tuple-element.654), channel_id=1, source_target_pairs={{0,8},{2,10},{4,12},{6,14},{8,0},{10,2},{12,4},{14,6},{1,9},{3,11}... | collective-permute-start | bytes 294920 | tf_op jit(solution)/shard_map/ppermute | solution.py:573
  45.2 10.8 %collective-permute-start.175 = (bf16[3,8,16,128]{3,2,1,0:T(8,128)(2,1)S(1)}, bf16[3,8,16,128]{3,2,1,0:T(8,128)(2,1)S(1)}, u32[]{:S(2)}, u32[]{:S(2)}) collective-permute-start(bf16[3,8,16,128]{3,2,1,0:T(8,128)(2,1)S(1)} %get-tuple-element.655), channel_id=1, source_target_pairs={{0,10},{2,12},{4,14},{6,0},{8,2},{10,4},{12,6},{14,8},{1,11},{3,13... | collective-permute-start | bytes 294920 | tf_op jit(solution)/shard_map/ppermute | solution.py:573
  46.8 9.4 %collective-permute-start.176 = (bf16[3,8,16,128]{3,2,1,0:T(8,128)(2,1)S(1)}, bf16[3,8,16,128]{3,2,1,0:T(8,128)(2,1)S(1)}, u32[]{:S(2)}, u32[]{:S(2)}) collective-permute-start(bf16[3,8,16,128]{3,2,1,0:T(8,128)(2,1)S(1)} %get-tuple-element.656), channel_id=1, source_target_pairs={{0,12},{2,14},{4,0},{6,2},{8,4},{10,6},{12,8},{14,10},{1,13},{3,15... | collective-permute-start | bytes 294920 | tf_op jit(solution)/shard_map/ppermute | solution.py:573
  46.8 14.3 %collective-permute-start.177 = (bf16[3,8,16,128]{3,2,1,0:T(8,128)(2,1)S(1)}, bf16[3,8,16,128]{3,2,1,0:T(8,128)(2,1)S(1)}, u32[]{:S(2)}, u32[]{:S(2)}) collective-permute-start(bf16[3,8,16,128]{3,2,1,0:T(8,128)(2,1)S(1)} %get-tuple-element.657), channel_id=1, source_target_pairs={{0,14},{2,0},{4,2},{6,4},{8,6},{10,8},{12,10},{14,12},{1,15},{3,1}... | collective-permute-start | bytes 294920 | tf_op jit(solution)/shard_map/ppermute | solution.py:573
  (2 other events, 12.3 us)
where the time goes:
time: 63.2 us; the launch traced here: 63 us
  waiting for transfers between devices  27.5 us (44%)
  Pallas kernels  22 us (35%)
  starting transfers between devices  10.1 us (16%)
  between operations  1.69 us (3%)
  local copies, waits for them, and re-layouts  0.78 us (1%)
    ppermute x10, waiting for transfers between devices, move(): lax.ppermute(block, 'pool', [(g, (g + v) % group_count) for g in range(gr...  24.4 us
    pallas_call x1, Pallas kernels, update(): pl.pallas_call(update_kernel, out_shape=(shape, shape), in_specs=[smem] *...  13.2 us
    ppermute x10, starting transfers between devices, move(): lax.ppermute(block, 'pool', [(g, (g + v) % group_count) for g in range(gr...  9.2 us
    pallas_call x1, Pallas kernels, project(): pl.pallas_call(project_kernel, out_shape=(pltpu.VMEM(out_shape, BF16), ja...  5.13 us
    pallas_call x1, Pallas kernels, exchange(): pl.pallas_call(functools.partial(pack_kernel, low, capacity), out_shape=[...  1.94 us
    pallas_call x1, Pallas kernels, exchange(): pl.pallas_call(functools.partial(unpack_kernel, low, capacity), out_shape...  1.69 us
    ppermute x1, waiting for transfers between devices, body(): other = lax.ppermute(send, 'dap', swap)  1.54 us
    ppermute x1, waiting for transfers between devices, body(): other_sides = lax.ppermute(send_sides, 'dap', swap)  1.49 us
  transfers between devices with their start and end apart: 13, of which 9 were waited for; matrix products, arithmetic and copies ran while one was open for 2% of the time, Pallas kernels for 8%

commit v1 on v0

--- a/solution.py
+++ b/solution.py
@@ -50,7 +50,6 @@
 
 
 def project_kernel(
-    place_ref,
     lengths_in,
     alignment_in,
     w_align_in,
@@ -69,7 +68,9 @@
     count = slots // 2
     inner = rights.shape[-1] // depth
     pieces = LANES // inner
-    half, theirs, mine, home = place_ref[0], place_ref[1], place_ref[2], place_ref[3]
+    half = lax.axis_index("dap")
+    mine, theirs = half * count, (1 - half) * count
+    home = lax.axis_index("pool") * slots
     copies = [
         pltpu.make_async_copy(source, target, sems.at[n])
         for n, (source, target) in enumerate(
@@ -138,7 +139,7 @@
             ]
 
 
-def project(place, lengths, alignment, w_align, w_spread):
+def project(lengths, alignment, w_align, w_spread):
     slots, depth, rows, _ = alignment.shape
     count = slots // 2
     inner = w_align.shape[0] // 2
@@ -149,7 +150,7 @@
     return pl.pallas_call(
         project_kernel,
         out_shape=(pltpu.VMEM(out_shape, BF16), jax.ShapeDtypeStruct(out_shape, BF16)),
-        in_specs=[smem, hbm, hbm, hbm, hbm],
+        in_specs=[hbm, hbm, hbm, hbm],
         out_specs=(vmem, vmem),
         scratch_shapes=[
             pltpu.SMEM(lengths.shape, jnp.int32),
@@ -163,11 +164,10 @@
         compiler_params=pltpu.CompilerParams(vmem_limit_bytes=PROJECT_LIMIT),
         cost_estimate=pl.CostEstimate(flops=2 * 10**9, bytes_accessed=4 * 10**6, transcendentals=0),
         name="project",
-    )(place, lengths, alignment, w_align, w_spread)
+    )(lengths, alignment, w_align, w_spread)
 
 
 def update_kernel(
-    place_ref,
     lengths_ref,
     breaks_ref,
     own_sides,
@@ -196,9 +196,9 @@
     pieces = LANES // inner
     sets = inner // pieces
     hidden = out_proj.shape[0]
-    half = place_ref[0]
-    start = place_ref[2]
-    home = place_ref[3] + start
+    half = lax.axis_index("dap")
+    start = half * count
+    home = lax.axis_index("pool") * pair.shape[0] + start
     low_is_own = half == 0
     groups = lane_groups(inner)
     zero = jnp.zeros((), BF16)
@@ -367,7 +367,7 @@
     round_of(list(range((rounds - 1) * ways, count)), [])
 
 
-def update(place, lengths, breaks, own_sides, other_sides, pair, other_pair, weights):
+def update(lengths, breaks, own_sides, other_sides, pair, other_pair, weights):
     outer_proj, chain_bias, out_ab, out_gate, out_proj, in_ab, in_gate, in_proj = weights
     count = own_sides.shape[0]
     _, full, width = pair.shape[1:]
@@ -378,7 +378,7 @@
     return pl.pallas_call(
         update_kernel,
         out_shape=(shape, shape),
-        in_specs=[smem] * 3 + [vmem] * 12,
+        in_specs=[smem] * 2 + [vmem] * 12,
         out_specs=(vmem, vmem),
         scratch_shapes=[
             pltpu.VMEM((width, width), BF16),
@@ -391,7 +391,6 @@
         cost_estimate=pl.CostEstimate(flops=10**10, bytes_accessed=4 * 10**6, transcendentals=0),
         name="pair_update",
     )(
-        place,
         lengths,
         breaks,
         own_sides,
@@ -451,13 +450,8 @@
     return [c for n in range(most + 1) for c in itertools.combinations(range(1, groups), n)]
 
 
-def pack_kernel(low, capacity, half_ref, shifts_ref, keep, other, *refs):
-    branch, table, counts, large = refs[-4:]
+def plan_kernel(low, capacity, shifts_ref, table, counts, large, branch):
     groups = counts.shape[0]
-    outs = refs[:-4]
-    statics, rests = outs[: groups - 1], outs[groups - 1 :]
-    count = keep.shape[0]
-    base = half_ref[0] * count
     build_tables(shifts_ref, table, counts, capacity)
     found = list_large(counts, large, low)
     taken = [large[k] for k in range(min(AT_ONCE, large.shape[0]))]
@@ -471,6 +465,14 @@
     branch[1] = found
     for k in range(AT_ONCE, large.shape[0]):
         branch[2 + k - AT_ONCE] = large[k]
+
+
+def pack_kernel(low, capacity, table, counts, large, branch, keep, other, *outs):
+    groups = counts.shape[0]
+    found = branch[1]
+    statics, rests = outs[: groups - 1], outs[groups - 1 :]
+    count = keep.shape[0]
+    base = lax.axis_index("dap") * count
 
     def fetch(v, rank):
         slot = jnp.where(rank < counts[v], table[v * capacity + rank], 0)
@@ -491,14 +493,13 @@
                 rest[rank - low] = fetch(v, rank)
 
 
-def unpack_kernel(low, capacity, half_ref, shifts_ref, keep, other, *refs):
-    out, table, counts, large, sem = refs[-5:]
+def unpack_kernel(low, capacity, table, counts, large, branch, keep, other, *refs):
     groups = counts.shape[0]
-    statics, rests = refs[: groups - 1], refs[groups - 1 : -5]
+    found = branch[1]
+    out, sem = refs[-2:]
+    statics, rests = refs[: groups - 1], refs[groups - 1 : -2]
     count = keep.shape[0]
-    base = half_ref[0] * count
-    build_tables(shifts_ref, table, counts, capacity)
-    found = list_large(counts, large, low)
+    base = lax.axis_index("dap") * count
 
     def put(source, slot):
         pltpu.make_async_copy(source, out.at[slot], sem).start()
@@ -536,38 +537,45 @@
     pltpu.make_async_copy(out, out, sem).wait()
 
 
-def exchange(half, shifts, keep, other, group_count, capacity):
-    slots = shifts.shape[0]
+def sizes(slots, group_count, capacity):
     low = capacity // 2
-    most = min(slots // (low + 1), group_count - 1)
-    most = max(most, AT_ONCE)
+    return low, max(min(slots // (low + 1), group_count - 1), AT_ONCE)
+
+
+def plan(shifts, group_count, capacity):
+    low, most = sizes(shifts.shape[0], group_count, capacity)
+    smem = pl.BlockSpec(memory_space=pltpu.SMEM)
+    lengths = (group_count * capacity, group_count, most, 2 + most - AT_ONCE)
+    return pl.pallas_call(
+        functools.partial(plan_kernel, low, capacity),
+        out_shape=[jax.ShapeDtypeStruct((length,), jnp.int32) for length in lengths],
+        in_specs=[smem],
+        out_specs=[smem] * 4,
+        cost_estimate=pl.CostEstimate(flops=10**6, bytes_accessed=10**6, transcendentals=0),
+        name="plan",
+    )(shifts)
+
+
+def exchange(tables, keep, other, slots, group_count, capacity):
+    low, most = sizes(slots, group_count, capacity)
+    branch = tables[-1]
     block = keep.shape[1:]
     smem = pl.BlockSpec(memory_space=pltpu.SMEM)
     vmem = pl.BlockSpec(memory_space=pltpu.VMEM)
     anywhere = pl.BlockSpec(memory_space=pl.ANY)
-    tables = [
-        pltpu.SMEM((group_count * capacity,), jnp.int32),
-        pltpu.SMEM((group_count,), jnp.int32),
-        pltpu.SMEM((most,), jnp.int32),
-        pltpu.SemaphoreType.DMA,
-    ]
     params = pltpu.CompilerParams(vmem_limit_bytes=VMEM_LIMIT)
     low_shape = jax.ShapeDtypeStruct((low,) + block, BF16)
     high_shape = jax.ShapeDtypeStruct((capacity - low,) + block, BF16)
     packed = pl.pallas_call(
         functools.partial(pack_kernel, low, capacity),
-        out_shape=[low_shape] * (group_count - 1)
-        + [high_shape] * most
-        + [jax.ShapeDtypeStruct((2 + most - AT_ONCE,), jnp.int32)],
-        in_specs=[smem, smem, vmem, vmem],
-        out_specs=[vmem] * (group_count - 1 + most) + [smem],
-        scratch_shapes=tables[:-1],
+        out_shape=[low_shape] * (group_count - 1) + [high_shape] * most,
+        in_specs=[smem] * 4 + [vmem, vmem],
+        out_specs=[vmem] * (group_count - 1 + most),
         compiler_params=params,
         name="pack",
-    )(half, shifts, keep, other)
+    )(*tables, keep, other)
     statics = packed[: group_count - 1]
-    rests = packed[group_count - 1 : -1]
-    branch = packed[-1]
+    rests = packed[group_count - 1 :]
 
     def move(block, v):
         return lax.ppermute(block, "pool", [(g, (g + v) % group_count) for g in range(group_count)])
@@ -599,12 +607,12 @@
     return pl.pallas_call(
         functools.partial(unpack_kernel, low, capacity),
         out_shape=jax.ShapeDtypeStruct((slots,) + block, BF16),
-        in_specs=[smem, smem] + [vmem] * (2 + group_count - 1 + most),
+        in_specs=[smem] * 4 + [vmem] * (2 + group_count - 1 + most),
         out_specs=anywhere,
-        scratch_shapes=tables,
+        scratch_shapes=[pltpu.SemaphoreType.DMA],
         compiler_params=params,
         name="unpack",
-    )(half, shifts, keep, other, *arrived, *late)
+    )(*tables, keep, other, *arrived, *late)
 
 
 def exchange_padded(half, shifts, keep, other, group_count, capacity):
@@ -629,12 +637,9 @@
 def body(pair_rep, alignment, lengths, chain_breaks, shifts, *weights):
     group_count = lax.axis_size("pool")
     slot_count = pair_rep.shape[0]
-    count = slot_count // 2
     capacity = max(2, (2 * slot_count + group_count - 1) // group_count)
     half = lax.axis_index("dap").astype(jnp.int32)
     swap = [(0, 1), (1, 0)]
-    place = jnp.stack([half, (1 - half) * count, half * count, lax.axis_index("pool") * slot_count])
-    place = place.astype(jnp.int32)
     alignment_proj, outer_proj = weights[:2]
     inner = alignment_proj.shape[1] // 2
     w_spread = spread_matrix(alignment.shape[1], inner)
@@ -642,14 +647,17 @@
         outer_proj.reshape(inner, inner, -1).transpose(1, 0, 2).reshape(outer_proj.shape)
     )
     other_pair = lax.ppermute(pair_rep, "dap", swap)
-    own_sides, send_sides = project(place, lengths, alignment, alignment_proj.T, w_spread)
+    own_sides, send_sides = project(lengths, alignment, alignment_proj.T, w_spread)
     other_sides = lax.ppermute(send_sides, "dap", swap)
     keep, send = update(
-        place, lengths, chain_breaks, own_sides, other_sides, pair_rep, other_pair, (w_outer,) + weights[2:]
+        lengths, chain_breaks, own_sides, other_sides, pair_rep, other_pair, (w_outer,) + weights[2:]
     )
+    if group_count > 8:
+        other = lax.ppermute(send, "dap", swap)
+        return exchange_padded(half, shifts, keep, other, group_count, capacity)
+    tables = plan(shifts, group_count, capacity)
     other = lax.ppermute(send, "dap", swap)
-    move = exchange if group_count <= 8 else exchange_padded
-    return move(half.reshape(1), shifts, keep, other, group_count, capacity)
+    return exchange(tables, keep, other, slot_count, group_count, capacity)
 
 
 def solution(mesh):

time: 63.2 us -> 62.3 us (0.986)
  waiting for transfers between devices: 27.5 us -> 25.5 us
  local copies, waits for them, and re-layouts: 0.78 us -> 2.78 us
    unnamed x26 -> x34, local copies, waits for them, and re-layouts: 0.07 us -> 1.99 us
    pallas_call x0 -> x1, Pallas kernels: none -> 1.67 us  [plan(): pl.pallas_call(functools.partial(plan_kernel, low, capacity), out_shape=[...]
    ppermute x1, waiting for transfers between devices: 1.54 us -> 0.01 us  [body(): other = lax.ppermute(send, 'dap', swap)]
    pallas_call x1, Pallas kernels: 1.94 us -> 0.97 us  [exchange(): pl.pallas_call(functools.partial(pack_kernel, low, capacity), out_shape=[...]
    pallas_call x1, Pallas kernels: 5.13 us -> 4.42 us  [project(): pl.pallas_call(project_kernel, out_shape=(pltpu.VMEM(out_shape, BF16), ja...]
  transfers between devices with their start and end apart: 13 -> 13, of which waited for: 9 -> 8; matrix products, arithmetic and copies ran while one was open for 2% -> 1% of each run, Pallas kernels for 8% -> 10%
where the time goes in v1:
time: 62.3 us; the launch traced here: 62.1 us
  waiting for transfers between devices  25.5 us (41%)
  Pallas kernels  21.6 us (35%)
  starting transfers between devices  10.2 us (16%)
  local copies, waits for them, and re-layouts  2.78 us (4%)
  between operations  1.75 us (3%)
    ppermute x10, waiting for transfers between devices, move(): lax.ppermute(block, 'pool', [(g, (g + v) % group_count) for g in range(gr...  24 us
    pallas_call x1, Pallas kernels, update(): pl.pallas_call(update_kernel, out_shape=(shape, shape), in_specs=[smem] *...  13.1 us
    ppermute x10, starting transfers between devices, move(): lax.ppermute(block, 'pool', [(g, (g + v) % group_count) for g in range(gr...  9.21 us
    pallas_call x1, Pallas kernels, project(): pl.pallas_call(project_kernel, out_shape=(pltpu.VMEM(out_shape, BF16), ja...  4.42 us
    unnamed x34, local copies, waits for them, and re-layouts  1.99 us
    pallas_call x1, Pallas kernels, plan(): pl.pallas_call(functools.partial(plan_kernel, low, capacity), out_shape=[...  1.67 us
    ppermute x1, waiting for transfers between devices, body(): other_sides = lax.ppermute(send_sides, 'dap', swap)  1.49 us
    pallas_call x1, Pallas kernels, exchange(): pl.pallas_call(functools.partial(unpack_kernel, low, capacity), out_shape...  1.43 us
  transfers between devices with their start and end apart: 13, of which 8 were waited for; matrix products, arithmetic and copies ran while one was open for 1% of the time, Pallas kernels for 10%

profile of v1, /device:TPU:15, one launch (start us, length us, event | category | flops | bytes accessed | tf_op | source)
XLA Modules:
  0.0 62.1 jit_solution(6672320453088869918)
XLA Ops:
  0.0 0.7 %collective-permute-start.169 = (bf16[22,8,16,128]{3,2,1,0:T(8,128)(2,1)}, bf16[22,8,16,128]{3,2,1,0:T(8,128)(2,1)S(1)}, u32[]{:S(2)}, u32[]{:S(2)}) collective-permute-start(bf16[22,8,16,128]{3,2,1,0:T(8,128)(2,1)} %pair.1), channel_id=1, source_target_pairs={{0,1},{1,0},{2,3},{3,2},{4,5},{5,4},{6,7},{7,6},{8,9},{9,8},{10,11... | collective-permute-start | bytes 2162696 | tf_op jit(solution)/shard_map/ppermute | solution.py:649
  0.8 4.4 %project.1 = (bf16[11,32,256]{2,1,0:T(8,128)(2,1)S(1)}, bf16[11,32,256]{2,1,0:T(8,128)(2,1)}) custom-call(s32[176]{0:T(256)} %lengths_ref.1, bf16[22,16,8,256]{3,2,1,0:T(8,128)(2,1)} %alignment_in.1, bf16[64,256]{1,0:T(8,128)(2,1)} %bitcast.11, bf16[512,512]{1,0:T(8,128)(2,1)} %constant.19.clone.w_spread_in), custom_call_target="tpu_custom_call" | custom-call | flops 2000000000 | bytes 4000000 | tf_op jit(solution)/shard_map/project/pallas_call | solution.py:150
  5.4 1.5 %collective-permute-done.168.other_sides = bf16[11,32,256]{2,1,0:T(8,128)(2,1)S(1)} collective-permute-done((bf16[11,32,256]{2,1,0:T(8,128)(2,1)}, bf16[11,32,256]{2,1,0:T(8,128)(2,1)S(1)}, u32[]{:S(2)}, u32[]{:S(2)}) %collective-permute-start.168) | collective-permute-done | bytes 180256 | tf_op jit(solution)/shard_map/ppermute | solution.py:651
  7.0 13.1 %pair_update.1 = (bf16[11,8,16,128]{3,2,1,0:T(8,128)(2,1)S(1)}, bf16[11,8,16,128]{3,2,1,0:T(8,128)(2,1)S(1)}) custom-call(s32[176]{0:T(256)S(1)} %copy-done.13, s32[176]{0:T(256)S(1)} %copy-done.14, bf16[11,32,256]{2,1,0:T(8,128)(2,1)S(1)} %get-tuple-element.654.own_sides, bf16[11,32,256]{2,1,0:T(8,128)(2,1)S(1)} %collective-permute-done.168.other_sides, ...), custom_call_target="tpu_custom_call" | custom-call | flops 10000000000 | bytes 4000000 | tf_op jit(solution)/shard_map/pair_update/pallas_call | solution.py:378
  20.3 1.7 %plan.1 = (s32[48]{0:T(128)}, s32[8]{0:T(128)}, s32[5]{0:T(128)}, s32[4]{0:T(128)S(1)}) custom-call(s32[22]{0:T(128)} %shifts_ref.1), custom_call_target="tpu_custom_call" | custom-call | flops 1000000 | bytes 1000000 | tf_op jit(solution)/shard_map/plan/pallas_call | solution.py:549
  22.0 0.6 %copy-done = s32[48]{0:T(128)S(1)} copy-done((s32[48]{0:T(128)S(1)}, s32[48]{0:T(128)}, u32[]{:S(2)}) %copy-start) | copy-done | bytes 216
  22.7 0.6 copy-done.2
  23.3 0.7 %copy-done.4 = s32[5]{0:T(128)S(1)} copy-done((s32[5]{0:T(128)S(1)}, s32[5]{0:T(128)}, u32[]{:S(2)}) %copy-start.4) | copy-done | bytes 44
  23.9 1.0 %pack.1 = (bf16[3,8,16,128]{3,2,1,0:T(8,128)(2,1)S(1)}, bf16[3,8,16,128]{3,2,1,0:T(8,128)(2,1)S(1)}, bf16[3,8,16,128]{3,2,1,0:T(8,128)(2,1)S(1)}, bf16[3,8,16,12...) custom-call(s32[48]{0:T(128)S(1)} %copy-done, ...), custom_call_target="tpu_custom_call" | custom-call | tf_op jit(solution)/shard_map/pack/pallas_call | solution.py:569
  24.9 1.3 %collective-permute-start.171 = (bf16[3,8,16,128]{3,2,1,0:T(8,128)(2,1)S(1)}, bf16[3,8,16,128]{3,2,1,0:T(8,128)(2,1)S(1)}, u32[]{:S(2)}, u32[]{:S(2)}) collective-permute-start(bf16[3,8,16,128]{3,2,1,0:T(8,128)(2,1)S(1)} %get-tuple-element.658), channel_id=1, source_target_pairs={{0,2},{2,4},{4,6},{6,8},{8,10},{10,12},{12,14},{14,0},{1,3},{3,5},... | collective-permute-start | bytes 294920 | tf_op jit(solution)/shard_map/ppermute | solution.py:581
  26.2 1.3 %collective-permute-start.172 = (bf16[3,8,16,128]{3,2,1,0:T(8,128)(2,1)S(1)}, bf16[3,8,16,128]{3,2,1,0:T(8,128)(2,1)S(1)}, u32[]{:S(2)}, u32[]{:S(2)}) collective-permute-start(bf16[3,8,16,128]{3,2,1,0:T(8,128)(2,1)S(1)} %get-tuple-element.659), channel_id=1, source_target_pairs={{0,4},{2,6},{4,8},{6,10},{8,12},{10,14},{12,0},{14,2},{1,5},{3,7},... | collective-permute-start | bytes 294920 | tf_op jit(solution)/shard_map/ppermute | solution.py:581
  27.5 0.7 %fusion.1 = (s32[1]{0:T(128)}, s32[1]{0:T(128)}) fusion(s32[4]{0:T(128)S(1)} %get-tuple-element.653.branch), kind=kLoop, calls=%fused_computation.1 | loop fusion | bytes 16 | tf_op jit(solution)/shard_map/slice | solution.py:606
  29.5 13.0 %conditional.4 = ((bf16[3,8,16,128]{3,2,1,0:T(8,128)(2,1)S(1)}, bf16[3,8,16,128]{3,2,1,0:T(8,128)(2,1)S(1)}, bf16[3,8,16,128]{3,2,1,0:T(8,128)(2,1)S(1)})) conditional(s32[]{:T(128)} %bitcast.6, (bf16[3,8,16,128]{3,2,1,0:T(8,128)(2,1)S(1)}, bf16[3,8,16,128]{3,2,1,0:T(8,128)(2,1)S(1)}, ...), branch_computations={%region_0.0_spmd, %region_1.0_spmd, %region_2.0_spmd, %region_3.0_... | conditional | bytes 1769624 | solution.py:596
  29.8 1.0 %collective-permute-start.127 = (bf16[3,8,16,128]{3,2,1,0:T(8,128)(2,1)S(1)}, bf16[3,8,16,128]{3,2,1,0:T(8,128)(2,1)S(1)}, u32[]{:S(2)}, u32[]{:S(2)}) collective-permute-start(bf16[3,8,16,128]{3,2,1,0:T(8,128)(2,1)S(1)} %get-tuple-element.595), channel_id=1, source_target_pairs={{0,6},{2,8},{4,10},{6,12},{8,14},{10,0},{12,2},{14,4},{1,7},{3,9},... | collective-permute-start | bytes 294920 | tf_op jit(solution)/shard_map/cond/branch_55_fun/ppermute | solution.py:581
  30.8 1.3 %collective-permute-start.128 = (bf16[3,8,16,128]{3,2,1,0:T(8,128)(2,1)S(1)}, bf16[3,8,16,128]{3,2,1,0:T(8,128)(2,1)S(1)}, u32[]{:S(2)}, u32[]{:S(2)}) collective-permute-start(bf16[3,8,16,128]{3,2,1,0:T(8,128)(2,1)S(1)} %get-tuple-element.596), channel_id=1, source_target_pairs={{0,8},{2,10},{4,12},{6,14},{8,0},{10,2},{12,4},{14,6},{1,9},{3,11}... | collective-permute-start | bytes 294920 | tf_op jit(solution)/shard_map/cond/branch_55_fun/ppermute | solution.py:581
  32.3 1.9 %collective-permute-done.127 = bf16[3,8,16,128]{3,2,1,0:T(8,128)(2,1)S(1)} collective-permute-done((bf16[3,8,16,128]{3,2,1,0:T(8,128)(2,1)S(1)}, bf16[3,8,16,128]{3,2,1,0:T(8,128)(2,1)S(1)}, u32[]{:S(2)}, u32[]{:S(2)}) %collective-permute-start.127) | collective-permute-done | bytes 98336 | tf_op jit(solution)/shard_map/cond/branch_55_fun/ppermute | solution.py:581
  34.2 6.7 %collective-permute-done.128 = bf16[3,8,16,128]{3,2,1,0:T(8,128)(2,1)S(1)} collective-permute-done((bf16[3,8,16,128]{3,2,1,0:T(8,128)(2,1)S(1)}, bf16[3,8,16,128]{3,2,1,0:T(8,128)(2,1)S(1)}, u32[]{:S(2)}, u32[]{:S(2)}) %collective-permute-start.128) | collective-permute-done | bytes 98336 | tf_op jit(solution)/shard_map/cond/branch_55_fun/ppermute | solution.py:581
  40.9 1.6 %collective-permute-done.129 = bf16[3,8,16,128]{3,2,1,0:T(8,128)(2,1)S(1)} collective-permute-done((bf16[3,8,16,128]{3,2,1,0:T(8,128)(2,1)S(1)}, bf16[3,8,16,128]{3,2,1,0:T(8,128)(2,1)S(1)}, u32[]{:S(2)}, u32[]{:S(2)}) %collective-permute-start.129) | collective-permute-done | bytes 98336 | tf_op jit(solution)/shard_map/cond/branch_55_fun/ppermute | solution.py:581
  42.7 2.4 %collective-permute-start.174 = (bf16[3,8,16,128]{3,2,1,0:T(8,128)(2,1)S(1)}, bf16[3,8,16,128]{3,2,1,0:T(8,128)(2,1)S(1)}, u32[]{:S(2)}, u32[]{:S(2)}) collective-permute-start(bf16[3,8,16,128]{3,2,1,0:T(8,128)(2,1)S(1)} %get-tuple-element.661), channel_id=1, source_target_pairs={{0,8},{2,10},{4,12},{6,14},{8,0},{10,2},{12,4},{14,6},{1,9},{3,11}... | collective-permute-start | bytes 294920 | tf_op jit(solution)/shard_map/ppermute | solution.py:581
  45.0 1.2 %collective-permute-start.175 = (bf16[3,8,16,128]{3,2,1,0:T(8,128)(2,1)S(1)}, bf16[3,8,16,128]{3,2,1,0:T(8,128)(2,1)S(1)}, u32[]{:S(2)}, u32[]{:S(2)}) collective-permute-start(bf16[3,8,16,128]{3,2,1,0:T(8,128)(2,1)S(1)} %get-tuple-element.662), channel_id=1, source_target_pairs={{0,10},{2,12},{4,14},{6,0},{8,2},{10,4},{12,6},{14,8},{1,11},{3,13... | collective-permute-start | bytes 294920 | tf_op jit(solution)/shard_map/ppermute | solution.py:581
  46.7 6.8 %collective-permute-done.173.refs_2_ = bf16[3,8,16,128]{3,2,1,0:T(8,128)(2,1)S(1)} collective-permute-done((bf16[3,8,16,128]{3,2,1,0:T(8,128)(2,1)S(1)}, bf16[3,8,16,128]{3,2,1,0:T(8,128)(2,1)S(1)}, u32[]{:S(2)}, u32[]{:S(2)}) %collective-permute-start.173) | collective-permute-done | bytes 98336 | tf_op jit(solution)/shard_map/ppermute | solution.py:581
  53.5 2.1 %collective-permute-done.174.refs_3_ = bf16[3,8,16,128]{3,2,1,0:T(8,128)(2,1)S(1)} collective-permute-done((bf16[3,8,16,128]{3,2,1,0:T(8,128)(2,1)S(1)}, bf16[3,8,16,128]{3,2,1,0:T(8,128)(2,1)S(1)}, u32[]{:S(2)}, u32[]{:S(2)}) %collective-permute-start.174) | collective-permute-done | bytes 98336 | tf_op jit(solution)/shard_map/ppermute | solution.py:581
  56.1 4.4 %collective-permute-done.177.refs_6_ = bf16[3,8,16,128]{3,2,1,0:T(8,128)(2,1)S(1)} collective-permute-done((bf16[3,8,16,128]{3,2,1,0:T(8,128)(2,1)S(1)}, bf16[3,8,16,128]{3,2,1,0:T(8,128)(2,1)S(1)}, u32[]{:S(2)}, u32[]{:S(2)}) %collective-permute-start.177) | collective-permute-done | bytes 98336 | tf_op jit(solution)/shard_map/ppermute | solution.py:581
  60.5 1.4 %unpack.1 = bf16[22,8,16,128]{3,2,1,0:T(8,128)(2,1)} custom-call(s32[48]{0:T(128)S(1)} %copy-done.1, s32[8]{0:T(128)S(1)} %copy-done.3, s32[5]{0:T(128)S(1)} %copy-done.5, s32[4]{0:T(128)S(1)} %get-tuple-element.653.branch, bf16[11,8,16,128]{3,2,1,0:T(8,128)(2,1)S(1)} %get-tuple-element.656.keep, ...), custom_call_target="tpu_custom_call" | custom-call | tf_op jit(solution)/shard_map/unpack/pallas_call | solution.py:607
  (48 shorter events, 1.7 us)
Async XLA Ops:
  0.0 6.9 %collective-permute-start.169 = (bf16[22,8,16,128]{3,2,1,0:T(8,128)(2,1)}, bf16[22,8,16,128]{3,2,1,0:T(8,128)(2,1)S(1)}, u32[]{:S(2)}, u32[]{:S(2)}) collective-permute-start(bf16[22,8,16,128]{3,2,1,0:T(8,128)(2,1)} %pair.1), channel_id=1, source_target_pairs={{0,1},{1,0},{2,3},{3,2},{4,5},{5,4},{6,7},{7,6},{8,9},{9,8},{10,11... | collective-permute-start | bytes 2162696 | tf_op jit(solution)/shard_map/ppermute | solution.py:649
  0.7 6.2 %copy-start.8 = (bf16[128,512]{1,0:T(8,128)(2,1)S(1)}, bf16[128,512]{1,0:T(8,128)(2,1)}, u32[]{:S(2)}) copy-start(bf16[128,512]{1,0:T(8,128)(2,1)} %in_ab.1) | copy-start | bytes 393220
  0.7 6.2 %copy-start.9 = (bf16[128,128]{1,0:T(8,128)(2,1)S(1)}, bf16[128,128]{1,0:T(8,128)(2,1)}, u32[]{:S(2)}) copy-start(bf16[128,128]{1,0:T(8,128)(2,1)} %out_gate.1) | copy-start | bytes 98308
  0.7 6.2 %copy-start.10 = (bf16[128,128]{1,0:T(8,128)(2,1)S(1)}, bf16[128,128]{1,0:T(8,128)(2,1)}, u32[]{:S(2)}) copy-start(bf16[128,128]{1,0:T(8,128)(2,1)} %out_proj.1) | copy-start | bytes 98308
  0.7 6.2 %copy-start.11 = (bf16[128,128]{1,0:T(8,128)(2,1)S(1)}, bf16[128,128]{1,0:T(8,128)(2,1)}, u32[]{:S(2)}) copy-start(bf16[128,128]{1,0:T(8,128)(2,1)} %in_gate.1) | copy-start | bytes 98308
  0.7 6.2 %copy-start.12 = (bf16[128,128]{1,0:T(8,128)(2,1)S(1)}, bf16[128,128]{1,0:T(8,128)(2,1)}, u32[]{:S(2)}) copy-start(bf16[128,128]{1,0:T(8,128)(2,1)} %in_proj.1) | copy-start | bytes 98308
  0.7 6.2 %copy-start.13 = (s32[176]{0:T(256)S(1)}, s32[176]{0:T(256)}, u32[]{:S(2)}) copy-start(s32[176]{0:T(256)} %lengths_ref.1) | copy-start | bytes 2116
  0.7 6.2 %copy-start.14 = (s32[176]{0:T(256)S(1)}, s32[176]{0:T(256)}, u32[]{:S(2)}) copy-start(s32[176]{0:T(256)} %breaks_ref.1) | copy-start | bytes 2116
  0.7 6.2 %copy-start.15 = (bf16[2,128]{1,0:T(2,128)(2,1)S(1)}, bf16[2,128]{1,0:T(2,128)(2,1)}, u32[]{:S(2)}) copy-start(bf16[2,128]{1,0:T(2,128)(2,1)} %bias.1) | copy-start | bytes 1540
  5.2 1.7 %collective-permute-start.168 = (bf16[11,32,256]{2,1,0:T(8,128)(2,1)}, bf16[11,32,256]{2,1,0:T(8,128)(2,1)S(1)}, u32[]{:S(2)}, u32[]{:S(2)}) collective-permute-start(bf16[11,32,256]{2,1,0:T(8,128)(2,1)} %get-tuple-element.655), channel_id=1, source_target_pairs={{0,1},{1,0},{2,3},{3,2},{4,5},{5,4},{6,7},{7,6},{8,9},{9,8},{10,11... | collective-permute-start | bytes 540680 | tf_op jit(solution)/shard_map/ppermute | solution.py:651
  20.1 1.9 %collective-permute-start.170 = (bf16[11,8,16,128]{3,2,1,0:T(8,128)(2,1)S(1)}, bf16[11,8,16,128]{3,2,1,0:T(8,128)(2,1)S(1)}, u32[]{:S(2)}, u32[]{:S(2)}) collective-permute-start(bf16[11,8,16,128]{3,2,1,0:T(8,128)(2,1)S(1)} %get-tuple-element.657), channel_id=1, source_target_pairs={{0,1},{1,0},{2,3},{3,2},{4,5},{5,4},{6,7},{7,6},{8,9},{9,8},{10,11... | collective-permute-start | bytes 1081352 | tf_op jit(solution)/shard_map/ppermute | solution.py:659
  24.9 21.3 %collective-permute-start.171 = (bf16[3,8,16,128]{3,2,1,0:T(8,128)(2,1)S(1)}, bf16[3,8,16,128]{3,2,1,0:T(8,128)(2,1)S(1)}, u32[]{:S(2)}, u32[]{:S(2)}) collective-permute-start(bf16[3,8,16,128]{3,2,1,0:T(8,128)(2,1)S(1)} %get-tuple-element.658), channel_id=1, source_target_pairs={{0,2},{2,4},{4,6},{6,8},{8,10},{10,12},{12,14},{14,0},{1,3},{3,5},... | collective-permute-start | bytes 294920 | tf_op jit(solution)/shard_map/ppermute | solution.py:581
  26.2 20.1 %collective-permute-start.172 = (bf16[3,8,16,128]{3,2,1,0:T(8,128)(2,1)S(1)}, bf16[3,8,16,128]{3,2,1,0:T(8,128)(2,1)S(1)}, u32[]{:S(2)}, u32[]{:S(2)}) collective-permute-start(bf16[3,8,16,128]{3,2,1,0:T(8,128)(2,1)S(1)} %get-tuple-element.659), channel_id=1, source_target_pairs={{0,4},{2,6},{4,8},{6,10},{8,12},{10,14},{12,0},{14,2},{1,5},{3,7},... | collective-permute-start | bytes 294920 | tf_op jit(solution)/shard_map/ppermute | solution.py:581
  29.8 4.4 %collective-permute-start.127 = (bf16[3,8,16,128]{3,2,1,0:T(8,128)(2,1)S(1)}, bf16[3,8,16,128]{3,2,1,0:T(8,128)(2,1)S(1)}, u32[]{:S(2)}, u32[]{:S(2)}) collective-permute-start(bf16[3,8,16,128]{3,2,1,0:T(8,128)(2,1)S(1)} %get-tuple-element.595), channel_id=1, source_target_pairs={{0,6},{2,8},{4,10},{6,12},{8,14},{10,0},{12,2},{14,4},{1,7},{3,9},... | collective-permute-start | bytes 294920 | tf_op jit(solution)/shard_map/cond/branch_55_fun/ppermute | solution.py:581
  30.8 10.1 %collective-permute-start.128 = (bf16[3,8,16,128]{3,2,1,0:T(8,128)(2,1)S(1)}, bf16[3,8,16,128]{3,2,1,0:T(8,128)(2,1)S(1)}, u32[]{:S(2)}, u32[]{:S(2)}) collective-permute-start(bf16[3,8,16,128]{3,2,1,0:T(8,128)(2,1)S(1)} %get-tuple-element.596), channel_id=1, source_target_pairs={{0,8},{2,10},{4,12},{6,14},{8,0},{10,2},{12,4},{14,6},{1,9},{3,11}... | collective-permute-start | bytes 294920 | tf_op jit(solution)/shard_map/cond/branch_55_fun/ppermute | solution.py:581
  32.2 10.4 %collective-permute-start.129 = (bf16[3,8,16,128]{3,2,1,0:T(8,128)(2,1)S(1)}, bf16[3,8,16,128]{3,2,1,0:T(8,128)(2,1)S(1)}, u32[]{:S(2)}, u32[]{:S(2)}) collective-permute-start(bf16[3,8,16,128]{3,2,1,0:T(8,128)(2,1)S(1)} %get-tuple-element.597), channel_id=1, source_target_pairs={{0,12},{2,14},{4,0},{6,2},{8,4},{10,6},{12,8},{14,10},{1,13},{3,15... | collective-permute-start | bytes 294920 | tf_op jit(solution)/shard_map/cond/branch_55_fun/ppermute | solution.py:581
  42.5 18.0 %copy-start.1 = (s32[48]{0:T(128)S(1)}, s32[48]{0:T(128)}, u32[]{:S(2)}) copy-start(s32[48]{0:T(128)} %get-tuple-element.650.table) | copy-start | bytes 580
  42.5 18.0 %copy-start.3 = (s32[8]{0:T(128)S(1)}, s32[8]{0:T(128)}, u32[]{:S(2)}) copy-start(s32[8]{0:T(128)} %get-tuple-element.651.counts) | copy-start | bytes 100
  42.6 18.0 %copy-start.5 = (s32[5]{0:T(128)S(1)}, s32[5]{0:T(128)}, u32[]{:S(2)}) copy-start(s32[5]{0:T(128)} %get-tuple-element.652.large) | copy-start | bytes 64
  42.6 10.9 %collective-permute-start.173 = (bf16[3,8,16,128]{3,2,1,0:T(8,128)(2,1)S(1)}, bf16[3,8,16,128]{3,2,1,0:T(8,128)(2,1)S(1)}, u32[]{:S(2)}, u32[]{:S(2)}) collective-permute-start(bf16[3,8,16,128]{3,2,1,0:T(8,128)(2,1)S(1)} %get-tuple-element.660), channel_id=1, source_target_pairs={{0,6},{2,8},{4,10},{6,12},{8,14},{10,0},{12,2},{14,4},{1,7},{3,9},... | collective-permute-start | bytes 294920 | tf_op jit(solution)/shard_map/ppermute | solution.py:581
  42.7 12.9 %collective-permute-start.174 = (bf16[3,8,16,128]{3,2,1,0:T(8,128)(2,1)S(1)}, bf16[3,8,16,128]{3,2,1,0:T(8,128)(2,1)S(1)}, u32[]{:S(2)}, u32[]{:S(2)}) collective-permute-start(bf16[3,8,16,128]{3,2,1,0:T(8,128)(2,1)S(1)} %get-tuple-element.661), channel_id=1, source_target_pairs={{0,8},{2,10},{4,12},{6,14},{8,0},{10,2},{12,4},{14,6},{1,9},{3,11}... | collective-permute-start | bytes 294920 | tf_op jit(solution)/shard_map/ppermute | solution.py:581
  45.0 10.5 %collective-permute-start.175 = (bf16[3,8,16,128]{3,2,1,0:T(8,128)(2,1)S(1)}, bf16[3,8,16,128]{3,2,1,0:T(8,128)(2,1)S(1)}, u32[]{:S(2)}, u32[]{:S(2)}) collective-permute-start(bf16[3,8,16,128]{3,2,1,0:T(8,128)(2,1)S(1)} %get-tuple-element.662), channel_id=1, source_target_pairs={{0,10},{2,12},{4,14},{6,0},{8,2},{10,4},{12,6},{14,8},{1,11},{3,13... | collective-permute-start | bytes 294920 | tf_op jit(solution)/shard_map/ppermute | solution.py:581
  46.2 9.8 %collective-permute-start.176 = (bf16[3,8,16,128]{3,2,1,0:T(8,128)(2,1)S(1)}, bf16[3,8,16,128]{3,2,1,0:T(8,128)(2,1)S(1)}, u32[]{:S(2)}, u32[]{:S(2)}) collective-permute-start(bf16[3,8,16,128]{3,2,1,0:T(8,128)(2,1)S(1)} %get-tuple-element.663), channel_id=1, source_target_pairs={{0,12},{2,14},{4,0},{6,2},{8,4},{10,6},{12,8},{14,10},{1,13},{3,15... | collective-permute-start | bytes 294920 | tf_op jit(solution)/shard_map/ppermute | solution.py:581
  46.3 14.2 %collective-permute-start.177 = (bf16[3,8,16,128]{3,2,1,0:T(8,128)(2,1)S(1)}, bf16[3,8,16,128]{3,2,1,0:T(8,128)(2,1)S(1)}, u32[]{:S(2)}, u32[]{:S(2)}) collective-permute-start(bf16[3,8,16,128]{3,2,1,0:T(8,128)(2,1)S(1)} %get-tuple-element.664), channel_id=1, source_target_pairs={{0,14},{2,0},{4,2},{6,4},{8,6},{10,8},{12,10},{14,12},{1,15},{3,1}... | collective-permute-start | bytes 294920 | tf_op jit(solution)/shard_map/ppermute | solution.py:581
  (6 other events, 19.0 us)

commit v2 on v1

--- a/solution.py
+++ b/solution.py
@@ -450,8 +450,20 @@
     return [c for n in range(most + 1) for c in itertools.combinations(range(1, groups), n)]
 
 
-def plan_kernel(low, capacity, shifts_ref, table, counts, large, branch):
-    groups = counts.shape[0]
+def split_plan(plan_ref, groups, capacity, most):
+    views, start = [], 0
+    for length in plan_lengths(groups, capacity, most):
+        views.append(plan_ref.at[pl.ds(start, length)])
+        start += length
+    return views
+
+
+def plan_lengths(groups, capacity, most):
+    return groups * capacity, groups, most, 2 + most - AT_ONCE
+
+
+def plan_kernel(low, capacity, groups, most, shifts_ref, plan_ref):
+    table, counts, large, branch = split_plan(plan_ref, groups, capacity, most)
     build_tables(shifts_ref, table, counts, capacity)
     found = list_large(counts, large, low)
     taken = [large[k] for k in range(min(AT_ONCE, large.shape[0]))]
@@ -467,8 +479,8 @@
         branch[2 + k - AT_ONCE] = large[k]
 
 
-def pack_kernel(low, capacity, table, counts, large, branch, keep, other, *outs):
-    groups = counts.shape[0]
+def pack_kernel(low, capacity, groups, most, plan_ref, keep, other, *outs):
+    table, counts, large, branch = split_plan(plan_ref, groups, capacity, most)
     found = branch[1]
     statics, rests = outs[: groups - 1], outs[groups - 1 :]
     count = keep.shape[0]
@@ -493,8 +505,8 @@
                 rest[rank - low] = fetch(v, rank)
 
 
-def unpack_kernel(low, capacity, table, counts, large, branch, keep, other, *refs):
-    groups = counts.shape[0]
+def unpack_kernel(low, capacity, groups, most, plan_ref, keep, other, *refs):
+    table, counts, large, branch = split_plan(plan_ref, groups, capacity, most)
     found = branch[1]
     out, sem = refs[-2:]
     statics, rests = refs[: groups - 1], refs[groups - 1 : -2]
@@ -545,12 +557,12 @@
 def plan(shifts, group_count, capacity):
     low, most = sizes(shifts.shape[0], group_count, capacity)
     smem = pl.BlockSpec(memory_space=pltpu.SMEM)
-    lengths = (group_count * capacity, group_count, most, 2 + most - AT_ONCE)
+    length = sum(plan_lengths(group_count, capacity, most))
     return pl.pallas_call(
-        functools.partial(plan_kernel, low, capacity),
-        out_shape=[jax.ShapeDtypeStruct((length,), jnp.int32) for length in lengths],
+        functools.partial(plan_kernel, low, capacity, group_count, most),
+        out_shape=jax.ShapeDtypeStruct((length,), jnp.int32),
         in_specs=[smem],
-        out_specs=[smem] * 4,
+        out_specs=smem,
         cost_estimate=pl.CostEstimate(flops=10**6, bytes_accessed=10**6, transcendentals=0),
         name="plan",
     )(shifts)
@@ -558,7 +570,7 @@
 
 def exchange(tables, keep, other, slots, group_count, capacity):
     low, most = sizes(slots, group_count, capacity)
-    branch = tables[-1]
+    branch = tables[sum(plan_lengths(group_count, capacity, most)[:-1]) :]
     block = keep.shape[1:]
     smem = pl.BlockSpec(memory_space=pltpu.SMEM)
     vmem = pl.BlockSpec(memory_space=pltpu.VMEM)
@@ -567,13 +579,13 @@
     low_shape = jax.ShapeDtypeStruct((low,) + block, BF16)
     high_shape = jax.ShapeDtypeStruct((capacity - low,) + block, BF16)
     packed = pl.pallas_call(
-        functools.partial(pack_kernel, low, capacity),
+        functools.partial(pack_kernel, low, capacity, group_count, most),
         out_shape=[low_shape] * (group_count - 1) + [high_shape] * most,
-        in_specs=[smem] * 4 + [vmem, vmem],
+        in_specs=[smem, vmem, vmem],
         out_specs=[vmem] * (group_count - 1 + most),
         compiler_params=params,
         name="pack",
-    )(*tables, keep, other)
+    )(tables, keep, other)
     statics = packed[: group_count - 1]
     rests = packed[group_count - 1 :]
 
@@ -605,14 +617,14 @@
 
         late += lax.cond(branch[1] > AT_ONCE, more, lambda *blocks: blocks, *rests[AT_ONCE:])
     return pl.pallas_call(
-        functools.partial(unpack_kernel, low, capacity),
+        functools.partial(unpack_kernel, low, capacity, group_count, most),
         out_shape=jax.ShapeDtypeStruct((slots,) + block, BF16),
-        in_specs=[smem] * 4 + [vmem] * (2 + group_count - 1 + most),
+        in_specs=[smem] + [vmem] * (2 + group_count - 1 + most),
         out_specs=anywhere,
         scratch_shapes=[pltpu.SemaphoreType.DMA],
         compiler_params=params,
         name="unpack",
-    )(*tables, keep, other, *arrived, *late)
+    )(tables, keep, other, *arrived, *late)
 
 
 def exchange_padded(half, shifts, keep, other, group_count, capacity):
@@ -648,6 +660,7 @@
     )
     other_pair = lax.ppermute(pair_rep, "dap", swap)
     own_sides, send_sides = project(lengths, alignment, alignment_proj.T, w_spread)
+    tables = plan(shifts, group_count, capacity) if group_count <= 8 else None
     other_sides = lax.ppermute(send_sides, "dap", swap)
     keep, send = update(
         lengths, chain_breaks, own_sides, other_sides, pair_rep, other_pair, (w_outer,) + weights[2:]
@@ -655,7 +668,6 @@
     if group_count > 8:
         other = lax.ppermute(send, "dap", swap)
         return exchange_padded(half, shifts, keep, other, group_count, capacity)
-    tables = plan(shifts, group_count, capacity)
     other = lax.ppermute(send, "dap", swap)
     return exchange(tables, keep, other, slot_count, group_count, capacity)
 

time: 62.3 us -> 60.5 us (0.971)
  local copies, waits for them, and re-layouts: 2.78 us -> 0.81 us
    unnamed x34 -> x22, local copies, waits for them, and re-layouts: 1.99 us -> 0.05 us
where the time goes in v2:
time: 60.5 us; the launch traced here: 60.3 us
  waiting for transfers between devices  26 us (43%)
  Pallas kernels  21.6 us (36%)
  starting transfers between devices  10 us (17%)
  between operations  1.67 us (3%)
  local copies, waits for them, and re-layouts  0.81 us (1%)
    ppermute x10, waiting for transfers between devices, move(): lax.ppermute(block, 'pool', [(g, (g + v) % group_count) for g in range(gr...  24.5 us
    pallas_call x1, Pallas kernels, update(): pl.pallas_call(update_kernel, out_shape=(shape, shape), in_specs=[smem] *...  13.1 us
    ppermute x10, starting transfers between devices, move(): lax.ppermute(block, 'pool', [(g, (g + v) % group_count) for g in range(gr...  9.05 us
    pallas_call x1, Pallas kernels, project(): pl.pallas_call(project_kernel, out_shape=(pltpu.VMEM(out_shape, BF16), ja...  4.42 us
    pallas_call x1, Pallas kernels, plan(): pl.pallas_call(functools.partial(plan_kernel, low, capacity, group_count,...  1.67 us
    ppermute x1, waiting for transfers between devices, body(): other_sides = lax.ppermute(send_sides, 'dap', swap)  1.49 us
    pallas_call x1, Pallas kernels, exchange(): pl.pallas_call(functools.partial(unpack_kernel, low, capacity, group_coun...  1.39 us
  transfers between devices with their start and end apart: 13, of which 8 were waited for; matrix products, arithmetic and copies ran while one was open for 1% of the time, Pallas kernels for 10%

profile of v2, /device:TPU:15, one launch (start us, length us, event | category | flops | bytes accessed | tf_op | source)
XLA Modules:
  0.0 60.3 jit_solution(14316196833543502858)
XLA Ops:
  0.0 0.7 %collective-permute-start.169 = (bf16[22,8,16,128]{3,2,1,0:T(8,128)(2,1)}, bf16[22,8,16,128]{3,2,1,0:T(8,128)(2,1)S(1)}, u32[]{:S(2)}, u32[]{:S(2)}) collective-permute-start(bf16[22,8,16,128]{3,2,1,0:T(8,128)(2,1)} %pair.1), channel_id=1, source_target_pairs={{0,1},{1,0},{2,3},{3,2},{4,5},{5,4},{6,7},{7,6},{8,9},{9,8},{10,11... | collective-permute-start | bytes 2162696 | tf_op jit(solution)/shard_map/ppermute | solution.py:661
  0.8 4.4 %project.1 = (bf16[11,32,256]{2,1,0:T(8,128)(2,1)S(1)}, bf16[11,32,256]{2,1,0:T(8,128)(2,1)}) custom-call(s32[176]{0:T(256)} %lengths_ref.1, bf16[22,16,8,256]{3,2,1,0:T(8,128)(2,1)} %alignment_in.1, bf16[64,256]{1,0:T(8,128)(2,1)} %bitcast.11, bf16[512,512]{1,0:T(8,128)(2,1)} %constant.19.clone.w_spread_in), custom_call_target="tpu_custom_call" | custom-call | flops 2000000000 | bytes 4000000 | tf_op jit(solution)/shard_map/project/pallas_call | solution.py:150
  5.4 1.5 %collective-permute-done.168.other_sides = bf16[11,32,256]{2,1,0:T(8,128)(2,1)S(1)} collective-permute-done((bf16[11,32,256]{2,1,0:T(8,128)(2,1)}, bf16[11,32,256]{2,1,0:T(8,128)(2,1)S(1)}, u32[]{:S(2)}, u32[]{:S(2)}) %collective-permute-start.168) | collective-permute-done | bytes 180256 | tf_op jit(solution)/shard_map/ppermute | solution.py:664
  7.0 13.1 %pair_update.1 = (bf16[11,8,16,128]{3,2,1,0:T(8,128)(2,1)S(1)}, bf16[11,8,16,128]{3,2,1,0:T(8,128)(2,1)S(1)}) custom-call(s32[176]{0:T(256)S(1)} %copy-done.7, s32[176]{0:T(256)S(1)} %copy-done.8, bf16[11,32,256]{2,1,0:T(8,128)(2,1)S(1)} %get-tuple-element.647.own_sides, bf16[11,32,256]{2,1,0:T(8,128)(2,1)S(1)} %collective-permute-done.168.other_sides, ...), custom_call_target="tpu_custom_call" | custom-call | flops 10000000000 | bytes 4000000 | tf_op jit(solution)/shard_map/pair_update/pallas_call | solution.py:378
  20.1 0.2 collective-permute-start.170
  20.3 1.7 %plan.1.plan_ref = s32[65]{0:T(128)S(1)} custom-call(s32[22]{0:T(128)} %shifts_ref.1), custom_call_target="tpu_custom_call" | custom-call | flops 1000000 | bytes 1000000 | tf_op jit(solution)/shard_map/plan/pallas_call | solution.py:561
  22.0 1.0 %pack.1 = (bf16[3,8,16,128]{3,2,1,0:T(8,128)(2,1)S(1)}, bf16[3,8,16,128]{3,2,1,0:T(8,128)(2,1)S(1)}, bf16[3,8,16,128]{3,2,1,0:T(8,128)(2,1)S(1)}, bf16[3,8,16,12...) custom-call(s32[65]{0:T(128)S(1)} %plan.1.plan_ref, ...), custom_call_target="tpu_custom_call" | custom-call | tf_op jit(solution)/shard_map/pack/pallas_call | solution.py:581
  23.0 1.3 %collective-permute-start.171 = (bf16[3,8,16,128]{3,2,1,0:T(8,128)(2,1)S(1)}, bf16[3,8,16,128]{3,2,1,0:T(8,128)(2,1)S(1)}, u32[]{:S(2)}, u32[]{:S(2)}) collective-permute-start(bf16[3,8,16,128]{3,2,1,0:T(8,128)(2,1)S(1)} %get-tuple-element.651), channel_id=1, source_target_pairs={{0,2},{2,4},{4,6},{6,8},{8,10},{10,12},{12,14},{14,0},{1,3},{3,5},... | collective-permute-start | bytes 294920 | tf_op jit(solution)/shard_map/ppermute | solution.py:593
  24.3 1.3 %collective-permute-start.172 = (bf16[3,8,16,128]{3,2,1,0:T(8,128)(2,1)S(1)}, bf16[3,8,16,128]{3,2,1,0:T(8,128)(2,1)S(1)}, u32[]{:S(2)}, u32[]{:S(2)}) collective-permute-start(bf16[3,8,16,128]{3,2,1,0:T(8,128)(2,1)S(1)} %get-tuple-element.652), channel_id=1, source_target_pairs={{0,4},{2,6},{4,8},{6,10},{8,12},{10,14},{12,0},{14,2},{1,5},{3,7},... | collective-permute-start | bytes 294920 | tf_op jit(solution)/shard_map/ppermute | solution.py:593
  25.6 0.6 %fusion.1 = (s32[1]{0:T(128)}, s32[1]{0:T(128)}) fusion(s32[65]{0:T(128)S(1)} %plan.1.plan_ref), kind=kLoop, calls=%fused_computation.1 | loop fusion | bytes 16 | tf_op jit(solution)/shard_map/slice | solution.py:618
  27.5 13.2 %conditional.4 = ((bf16[3,8,16,128]{3,2,1,0:T(8,128)(2,1)S(1)}, bf16[3,8,16,128]{3,2,1,0:T(8,128)(2,1)S(1)}, bf16[3,8,16,128]{3,2,1,0:T(8,128)(2,1)S(1)})) conditional(s32[]{:T(128)} %bitcast.6, (bf16[3,8,16,128]{3,2,1,0:T(8,128)(2,1)S(1)}, bf16[3,8,16,128]{3,2,1,0:T(8,128)(2,1)S(1)}, ...), branch_computations={%region_0.0_spmd, %region_1.0_spmd, %region_2.0_spmd, %region_3.0_... | conditional | bytes 1769624 | solution.py:608
  27.8 1.0 %collective-permute-start.127 = (bf16[3,8,16,128]{3,2,1,0:T(8,128)(2,1)S(1)}, bf16[3,8,16,128]{3,2,1,0:T(8,128)(2,1)S(1)}, u32[]{:S(2)}, u32[]{:S(2)}) collective-permute-start(bf16[3,8,16,128]{3,2,1,0:T(8,128)(2,1)S(1)} %get-tuple-element.596), channel_id=1, source_target_pairs={{0,6},{2,8},{4,10},{6,12},{8,14},{10,0},{12,2},{14,4},{1,7},{3,9},... | collective-permute-start | bytes 294920 | tf_op jit(solution)/shard_map/cond/branch_55_fun/ppermute | solution.py:593
  28.8 1.3 %collective-permute-start.128 = (bf16[3,8,16,128]{3,2,1,0:T(8,128)(2,1)S(1)}, bf16[3,8,16,128]{3,2,1,0:T(8,128)(2,1)S(1)}, u32[]{:S(2)}, u32[]{:S(2)}) collective-permute-start(bf16[3,8,16,128]{3,2,1,0:T(8,128)(2,1)S(1)} %get-tuple-element.597), channel_id=1, source_target_pairs={{0,8},{2,10},{4,12},{6,14},{8,0},{10,2},{12,4},{14,6},{1,9},{3,11}... | collective-permute-start | bytes 294920 | tf_op jit(solution)/shard_map/cond/branch_55_fun/ppermute | solution.py:593
  30.3 1.9 %collective-permute-done.127 = bf16[3,8,16,128]{3,2,1,0:T(8,128)(2,1)S(1)} collective-permute-done((bf16[3,8,16,128]{3,2,1,0:T(8,128)(2,1)S(1)}, bf16[3,8,16,128]{3,2,1,0:T(8,128)(2,1)S(1)}, u32[]{:S(2)}, u32[]{:S(2)}) %collective-permute-start.127) | collective-permute-done | bytes 98336 | tf_op jit(solution)/shard_map/cond/branch_55_fun/ppermute | solution.py:593
  32.2 6.7 %collective-permute-done.128 = bf16[3,8,16,128]{3,2,1,0:T(8,128)(2,1)S(1)} collective-permute-done((bf16[3,8,16,128]{3,2,1,0:T(8,128)(2,1)S(1)}, bf16[3,8,16,128]{3,2,1,0:T(8,128)(2,1)S(1)}, u32[]{:S(2)}, u32[]{:S(2)}) %collective-permute-start.128) | collective-permute-done | bytes 98336 | tf_op jit(solution)/shard_map/cond/branch_55_fun/ppermute | solution.py:593
  38.9 1.7 %collective-permute-done.129 = bf16[3,8,16,128]{3,2,1,0:T(8,128)(2,1)S(1)} collective-permute-done((bf16[3,8,16,128]{3,2,1,0:T(8,128)(2,1)S(1)}, bf16[3,8,16,128]{3,2,1,0:T(8,128)(2,1)S(1)}, u32[]{:S(2)}, u32[]{:S(2)}) %collective-permute-start.129) | collective-permute-done | bytes 98336 | tf_op jit(solution)/shard_map/cond/branch_55_fun/ppermute | solution.py:593
  40.7 2.3 %collective-permute-start.174 = (bf16[3,8,16,128]{3,2,1,0:T(8,128)(2,1)S(1)}, bf16[3,8,16,128]{3,2,1,0:T(8,128)(2,1)S(1)}, u32[]{:S(2)}, u32[]{:S(2)}) collective-permute-start(bf16[3,8,16,128]{3,2,1,0:T(8,128)(2,1)S(1)} %get-tuple-element.654), channel_id=1, source_target_pairs={{0,8},{2,10},{4,12},{6,14},{8,0},{10,2},{12,4},{14,6},{1,9},{3,11}... | collective-permute-start | bytes 294920 | tf_op jit(solution)/shard_map/ppermute | solution.py:593
  43.0 1.2 %collective-permute-start.175 = (bf16[3,8,16,128]{3,2,1,0:T(8,128)(2,1)S(1)}, bf16[3,8,16,128]{3,2,1,0:T(8,128)(2,1)S(1)}, u32[]{:S(2)}, u32[]{:S(2)}) collective-permute-start(bf16[3,8,16,128]{3,2,1,0:T(8,128)(2,1)S(1)} %get-tuple-element.655), channel_id=1, source_target_pairs={{0,10},{2,12},{4,14},{6,0},{8,2},{10,4},{12,6},{14,8},{1,11},{3,13... | collective-permute-start | bytes 294920 | tf_op jit(solution)/shard_map/ppermute | solution.py:593
  44.2 0.2 collective-permute-start.176
  44.6 7.0 %collective-permute-done.173.refs_2_ = bf16[3,8,16,128]{3,2,1,0:T(8,128)(2,1)S(1)} collective-permute-done((bf16[3,8,16,128]{3,2,1,0:T(8,128)(2,1)S(1)}, bf16[3,8,16,128]{3,2,1,0:T(8,128)(2,1)S(1)}, u32[]{:S(2)}, u32[]{:S(2)}) %collective-permute-start.173) | collective-permute-done | bytes 98336 | tf_op jit(solution)/shard_map/ppermute | solution.py:593
  51.6 2.1 %collective-permute-done.174.refs_3_ = bf16[3,8,16,128]{3,2,1,0:T(8,128)(2,1)S(1)} collective-permute-done((bf16[3,8,16,128]{3,2,1,0:T(8,128)(2,1)S(1)}, bf16[3,8,16,128]{3,2,1,0:T(8,128)(2,1)S(1)}, u32[]{:S(2)}, u32[]{:S(2)}) %collective-permute-start.174) | collective-permute-done | bytes 98336 | tf_op jit(solution)/shard_map/ppermute | solution.py:593
  53.7 0.3 collective-permute-done.176.refs_5_
  54.0 4.8 %collective-permute-done.177.refs_6_ = bf16[3,8,16,128]{3,2,1,0:T(8,128)(2,1)S(1)} collective-permute-done((bf16[3,8,16,128]{3,2,1,0:T(8,128)(2,1)S(1)}, bf16[3,8,16,128]{3,2,1,0:T(8,128)(2,1)S(1)}, u32[]{:S(2)}, u32[]{:S(2)}) %collective-permute-start.177) | collective-permute-done | bytes 98336 | tf_op jit(solution)/shard_map/ppermute | solution.py:593
  58.8 1.4 %unpack.1 = bf16[22,8,16,128]{3,2,1,0:T(8,128)(2,1)} custom-call(s32[65]{0:T(128)S(1)} %plan.1.plan_ref, bf16[11,8,16,128]{3,2,1,0:T(8,128)(2,1)S(1)} %get-tuple-element.649.keep, bf16[11,8,16,128]{3,2,1,0:T(8,128)(2,1)S(1)} %collective-permute-done.170.other, bf16[3,8,16,128]{3,2,1,0:T(8,128)(2,1)S(1)} %collective-permute-done.171.refs_0_, ...), custom_call_target="tpu_custom_call" | custom-call | tf_op jit(solution)/shard_map/unpack/pallas_call | solution.py:619
  (36 shorter events, 0.7 us)
Async XLA Ops:
  0.0 6.9 %collective-permute-start.169 = (bf16[22,8,16,128]{3,2,1,0:T(8,128)(2,1)}, bf16[22,8,16,128]{3,2,1,0:T(8,128)(2,1)S(1)}, u32[]{:S(2)}, u32[]{:S(2)}) collective-permute-start(bf16[22,8,16,128]{3,2,1,0:T(8,128)(2,1)} %pair.1), channel_id=1, source_target_pairs={{0,1},{1,0},{2,3},{3,2},{4,5},{5,4},{6,7},{7,6},{8,9},{9,8},{10,11... | collective-permute-start | bytes 2162696 | tf_op jit(solution)/shard_map/ppermute | solution.py:661
  0.7 4.6 %copy-start.10 = (bf16[1024,128]{1,0:T(8,128)(2,1)S(1)}, bf16[1024,128]{1,0:T(8,128)(2,1)}, u32[]{:S(2)}) copy-start(bf16[1024,128]{1,0:T(8,128)(2,1)} %param.103) | copy-start | bytes 786436
  0.7 6.2 %copy-start = (bf16[22,8,16,128]{3,2,1,0:T(8,128)(2,1)S(1)}, bf16[22,8,16,128]{3,2,1,0:T(8,128)(2,1)}, u32[]{:S(2)}) copy-start(bf16[22,8,16,128]{3,2,1,0:T(8,128)(2,1)} %pair.1) | copy-start | bytes 2162692
  0.7 6.2 %copy-start.1 = (bf16[128,512]{1,0:T(8,128)(2,1)S(1)}, bf16[128,512]{1,0:T(8,128)(2,1)}, u32[]{:S(2)}) copy-start(bf16[128,512]{1,0:T(8,128)(2,1)} %out_ab.1) | copy-start | bytes 393220
  0.7 6.2 %copy-start.2 = (bf16[128,512]{1,0:T(8,128)(2,1)S(1)}, bf16[128,512]{1,0:T(8,128)(2,1)}, u32[]{:S(2)}) copy-start(bf16[128,512]{1,0:T(8,128)(2,1)} %in_ab.1) | copy-start | bytes 393220
  0.7 6.2 %copy-start.3 = (bf16[128,128]{1,0:T(8,128)(2,1)S(1)}, bf16[128,128]{1,0:T(8,128)(2,1)}, u32[]{:S(2)}) copy-start(bf16[128,128]{1,0:T(8,128)(2,1)} %out_gate.1) | copy-start | bytes 98308
  0.7 6.2 %copy-start.4 = (bf16[128,128]{1,0:T(8,128)(2,1)S(1)}, bf16[128,128]{1,0:T(8,128)(2,1)}, u32[]{:S(2)}) copy-start(bf16[128,128]{1,0:T(8,128)(2,1)} %out_proj.1) | copy-start | bytes 98308
  0.7 6.2 %copy-start.5 = (bf16[128,128]{1,0:T(8,128)(2,1)S(1)}, bf16[128,128]{1,0:T(8,128)(2,1)}, u32[]{:S(2)}) copy-start(bf16[128,128]{1,0:T(8,128)(2,1)} %in_gate.1) | copy-start | bytes 98308
  0.7 6.2 %copy-start.6 = (bf16[128,128]{1,0:T(8,128)(2,1)S(1)}, bf16[128,128]{1,0:T(8,128)(2,1)}, u32[]{:S(2)}) copy-start(bf16[128,128]{1,0:T(8,128)(2,1)} %in_proj.1) | copy-start | bytes 98308
  0.7 6.2 %copy-start.7 = (s32[176]{0:T(256)S(1)}, s32[176]{0:T(256)}, u32[]{:S(2)}) copy-start(s32[176]{0:T(256)} %lengths_ref.1) | copy-start | bytes 2116
  0.7 6.2 %copy-start.8 = (s32[176]{0:T(256)S(1)}, s32[176]{0:T(256)}, u32[]{:S(2)}) copy-start(s32[176]{0:T(256)} %breaks_ref.1) | copy-start | bytes 2116
  0.7 6.2 %copy-start.9 = (bf16[2,128]{1,0:T(2,128)(2,1)S(1)}, bf16[2,128]{1,0:T(2,128)(2,1)}, u32[]{:S(2)}) copy-start(bf16[2,128]{1,0:T(2,128)(2,1)} %bias.1) | copy-start | bytes 1540
  5.2 1.7 %collective-permute-start.168 = (bf16[11,32,256]{2,1,0:T(8,128)(2,1)}, bf16[11,32,256]{2,1,0:T(8,128)(2,1)S(1)}, u32[]{:S(2)}, u32[]{:S(2)}) collective-permute-start(bf16[11,32,256]{2,1,0:T(8,128)(2,1)} %get-tuple-element.648), channel_id=1, source_target_pairs={{0,1},{1,0},{2,3},{3,2},{4,5},{5,4},{6,7},{7,6},{8,9},{9,8},{10,11... | collective-permute-start | bytes 540680 | tf_op jit(solution)/shard_map/ppermute | solution.py:664
  20.1 1.9 %collective-permute-start.170 = (bf16[11,8,16,128]{3,2,1,0:T(8,128)(2,1)S(1)}, bf16[11,8,16,128]{3,2,1,0:T(8,128)(2,1)S(1)}, u32[]{:S(2)}, u32[]{:S(2)}) collective-permute-start(bf16[11,8,16,128]{3,2,1,0:T(8,128)(2,1)S(1)} %get-tuple-element.650), channel_id=1, source_target_pairs={{0,1},{1,0},{2,3},{3,2},{4,5},{5,4},{6,7},{7,6},{8,9},{9,8},{10,11... | collective-permute-start | bytes 1081352 | tf_op jit(solution)/shard_map/ppermute | solution.py:671
  23.0 21.2 %collective-permute-start.171 = (bf16[3,8,16,128]{3,2,1,0:T(8,128)(2,1)S(1)}, bf16[3,8,16,128]{3,2,1,0:T(8,128)(2,1)S(1)}, u32[]{:S(2)}, u32[]{:S(2)}) collective-permute-start(bf16[3,8,16,128]{3,2,1,0:T(8,128)(2,1)S(1)} %get-tuple-element.651), channel_id=1, source_target_pairs={{0,2},{2,4},{4,6},{6,8},{8,10},{10,12},{12,14},{14,0},{1,3},{3,5},... | collective-permute-start | bytes 294920 | tf_op jit(solution)/shard_map/ppermute | solution.py:593
  24.3 20.2 %collective-permute-start.172 = (bf16[3,8,16,128]{3,2,1,0:T(8,128)(2,1)S(1)}, bf16[3,8,16,128]{3,2,1,0:T(8,128)(2,1)S(1)}, u32[]{:S(2)}, u32[]{:S(2)}) collective-permute-start(bf16[3,8,16,128]{3,2,1,0:T(8,128)(2,1)S(1)} %get-tuple-element.652), channel_id=1, source_target_pairs={{0,4},{2,6},{4,8},{6,10},{8,12},{10,14},{12,0},{14,2},{1,5},{3,7},... | collective-permute-start | bytes 294920 | tf_op jit(solution)/shard_map/ppermute | solution.py:593
  27.8 4.4 %collective-permute-start.127 = (bf16[3,8,16,128]{3,2,1,0:T(8,128)(2,1)S(1)}, bf16[3,8,16,128]{3,2,1,0:T(8,128)(2,1)S(1)}, u32[]{:S(2)}, u32[]{:S(2)}) collective-permute-start(bf16[3,8,16,128]{3,2,1,0:T(8,128)(2,1)S(1)} %get-tuple-element.596), channel_id=1, source_target_pairs={{0,6},{2,8},{4,10},{6,12},{8,14},{10,0},{12,2},{14,4},{1,7},{3,9},... | collective-permute-start | bytes 294920 | tf_op jit(solution)/shard_map/cond/branch_55_fun/ppermute | solution.py:593
  28.8 10.1 %collective-permute-start.128 = (bf16[3,8,16,128]{3,2,1,0:T(8,128)(2,1)S(1)}, bf16[3,8,16,128]{3,2,1,0:T(8,128)(2,1)S(1)}, u32[]{:S(2)}, u32[]{:S(2)}) collective-permute-start(bf16[3,8,16,128]{3,2,1,0:T(8,128)(2,1)S(1)} %get-tuple-element.597), channel_id=1, source_target_pairs={{0,8},{2,10},{4,12},{6,14},{8,0},{10,2},{12,4},{14,6},{1,9},{3,11}... | collective-permute-start | bytes 294920 | tf_op jit(solution)/shard_map/cond/branch_55_fun/ppermute | solution.py:593
  30.1 10.5 %collective-permute-start.129 = (bf16[3,8,16,128]{3,2,1,0:T(8,128)(2,1)S(1)}, bf16[3,8,16,128]{3,2,1,0:T(8,128)(2,1)S(1)}, u32[]{:S(2)}, u32[]{:S(2)}) collective-permute-start(bf16[3,8,16,128]{3,2,1,0:T(8,128)(2,1)S(1)} %get-tuple-element.598), channel_id=1, source_target_pairs={{0,12},{2,14},{4,0},{6,2},{8,4},{10,6},{12,8},{14,10},{1,13},{3,15... | collective-permute-start | bytes 294920 | tf_op jit(solution)/shard_map/cond/branch_55_fun/ppermute | solution.py:593
  40.7 10.9 %collective-permute-start.173 = (bf16[3,8,16,128]{3,2,1,0:T(8,128)(2,1)S(1)}, bf16[3,8,16,128]{3,2,1,0:T(8,128)(2,1)S(1)}, u32[]{:S(2)}, u32[]{:S(2)}) collective-permute-start(bf16[3,8,16,128]{3,2,1,0:T(8,128)(2,1)S(1)} %get-tuple-element.653), channel_id=1, source_target_pairs={{0,6},{2,8},{4,10},{6,12},{8,14},{10,0},{12,2},{14,4},{1,7},{3,9},... | collective-permute-start | bytes 294920 | tf_op jit(solution)/shard_map/ppermute | solution.py:593
  40.7 13.0 %collective-permute-start.174 = (bf16[3,8,16,128]{3,2,1,0:T(8,128)(2,1)S(1)}, bf16[3,8,16,128]{3,2,1,0:T(8,128)(2,1)S(1)}, u32[]{:S(2)}, u32[]{:S(2)}) collective-permute-start(bf16[3,8,16,128]{3,2,1,0:T(8,128)(2,1)S(1)} %get-tuple-element.654), channel_id=1, source_target_pairs={{0,8},{2,10},{4,12},{6,14},{8,0},{10,2},{12,4},{14,6},{1,9},{3,11}... | collective-permute-start | bytes 294920 | tf_op jit(solution)/shard_map/ppermute | solution.py:593
  43.0 10.7 %collective-permute-start.175 = (bf16[3,8,16,128]{3,2,1,0:T(8,128)(2,1)S(1)}, bf16[3,8,16,128]{3,2,1,0:T(8,128)(2,1)S(1)}, u32[]{:S(2)}, u32[]{:S(2)}) collective-permute-start(bf16[3,8,16,128]{3,2,1,0:T(8,128)(2,1)S(1)} %get-tuple-element.655), channel_id=1, source_target_pairs={{0,10},{2,12},{4,14},{6,0},{8,2},{10,4},{12,6},{14,8},{1,11},{3,13... | collective-permute-start | bytes 294920 | tf_op jit(solution)/shard_map/ppermute | solution.py:593
  44.2 9.8 %collective-permute-start.176 = (bf16[3,8,16,128]{3,2,1,0:T(8,128)(2,1)S(1)}, bf16[3,8,16,128]{3,2,1,0:T(8,128)(2,1)S(1)}, u32[]{:S(2)}, u32[]{:S(2)}) collective-permute-start(bf16[3,8,16,128]{3,2,1,0:T(8,128)(2,1)S(1)} %get-tuple-element.656), channel_id=1, source_target_pairs={{0,12},{2,14},{4,0},{6,2},{8,4},{10,6},{12,8},{14,10},{1,13},{3,15... | collective-permute-start | bytes 294920 | tf_op jit(solution)/shard_map/ppermute | solution.py:593
  44.4 14.3 %collective-permute-start.177 = (bf16[3,8,16,128]{3,2,1,0:T(8,128)(2,1)S(1)}, bf16[3,8,16,128]{3,2,1,0:T(8,128)(2,1)S(1)}, u32[]{:S(2)}, u32[]{:S(2)}) collective-permute-start(bf16[3,8,16,128]{3,2,1,0:T(8,128)(2,1)S(1)} %get-tuple-element.657), channel_id=1, source_target_pairs={{0,14},{2,0},{4,2},{6,4},{8,6},{10,8},{12,10},{14,12},{1,15},{3,1}... | collective-permute-start | bytes 294920 | tf_op jit(solution)/shard_map/ppermute | solution.py:593

commit v3 on v2

--- a/solution.py
+++ b/solution.py
@@ -17,7 +17,7 @@
 VMEM_LIMIT = 24 * 2**20
 PROJECT_LIMIT = 64500000
 WAYS = 4
-PROJECT_WAYS = 3
+PROJECT_WAYS = 6
 OUTER_AFTER = 2
 BLOCK = 4
 OUTER_TILES = 4
@@ -354,7 +354,7 @@
     def round_of(steps, ahead):
         streams = [whole(step, way) for way, step in enumerate(steps)]
         outers = [outer_update(way, step) for way, step in enumerate(ahead)]
-        interleave(streams + [later(outers, OUTER_AFTER)])
+        interleave([later(outers, OUTER_AFTER)] + streams)
 
     def both(round_, carry):
         base = round_ * ways
@@ -568,9 +568,8 @@
     )(shifts)
 
 
-def exchange(tables, keep, other, slots, group_count, capacity):
+def exchange(picks, tables, keep, other, slots, group_count, capacity):
     low, most = sizes(slots, group_count, capacity)
-    branch = tables[sum(plan_lengths(group_count, capacity, most)[:-1]) :]
     block = keep.shape[1:]
     smem = pl.BlockSpec(memory_space=pltpu.SMEM)
     vmem = pl.BlockSpec(memory_space=pltpu.VMEM)
@@ -606,16 +605,16 @@
 
     late = list(
         lax.switch(
-            branch[0], [choice(subset) for subset in subsets(group_count, AT_ONCE)], *rests[:AT_ONCE]
+            picks[0], [choice(subset) for subset in subsets(group_count, AT_ONCE)], *rests[:AT_ONCE]
         )
     )
     if most > AT_ONCE:
 
         def more(*blocks):
             singles = [choice(subset) for subset in subsets(group_count, 1)]
-            return tuple(lax.switch(branch[2 + k], singles, block)[0] for k, block in enumerate(blocks))
-
-        late += lax.cond(branch[1] > AT_ONCE, more, lambda *blocks: blocks, *rests[AT_ONCE:])
+            return tuple(lax.switch(picks[2 + k], singles, block)[0] for k, block in enumerate(blocks))
+
+        late += lax.switch(picks[1], [lambda *blocks: blocks, more], *rests[AT_ONCE:])
     return pl.pallas_call(
         functools.partial(unpack_kernel, low, capacity, group_count, most),
         out_shape=jax.ShapeDtypeStruct((slots,) + block, BF16),
@@ -669,7 +668,12 @@
         other = lax.ppermute(send, "dap", swap)
         return exchange_padded(half, shifts, keep, other, group_count, capacity)
     other = lax.ppermute(send, "dap", swap)
-    return exchange(tables, keep, other, slot_count, group_count, capacity)
+    _, most = sizes(slot_count, group_count, capacity)
+    choices = tables[sum(plan_lengths(group_count, capacity, most)[:-1]) :]
+    picks = [choices[0], (choices[1] > AT_ONCE).astype(jnp.int32)]
+    picks += [choices[2 + k] for k in range(most - AT_ONCE)]
+    other, picks = lax.optimization_barrier((other, picks))
+    return exchange(picks, tables, keep, other, slot_count, group_count, capacity)
 
 
 def solution(mesh):

time: 60.5 us -> 63.8 us (1.055)
  local copies, waits for them, and re-layouts: 0.81 us -> 3.19 us
  waiting for transfers between devices: 26 us -> 28 us
  Pallas kernels: 21.6 us -> 20.6 us
    ppermute x10, waiting for transfers between devices: 24.5 us -> 26.5 us  [move(): lax.ppermute(block, 'pool', [(g, (g + v) % group_count) for g in range(gr...]
    unnamed x22 -> x26, local copies, waits for them, and re-layouts: 0.05 us -> 1.6 us
    slice x1, local copies, waits for them, and re-layouts: 0.64 us -> 1.46 us  [body(): picks += [choices[2 + k] for k in range(most - AT_ONCE)]]
  transfers between devices with their start and end apart: 13 -> 13, of which waited for: 8 -> 8; matrix products, arithmetic and copies ran while one was open for 1% -> 2% of each run, Pallas kernels for 10% -> 9%
where the time goes in v3:
time: 63.8 us; the launch traced here: 63.6 us
  waiting for transfers between devices  28 us (44%)
  Pallas kernels  20.6 us (32%)
  starting transfers between devices  9.82 us (15%)
  local copies, waits for them, and re-layouts  3.19 us (5%)
  between operations  1.67 us (3%)
    ppermute x10, waiting for transfers between devices, move(): lax.ppermute(block, 'pool', [(g, (g + v) % group_count) for g in range(gr...  26.5 us
    pallas_call x1, Pallas kernels, update(): pl.pallas_call(update_kernel, out_shape=(shape, shape), in_specs=[smem] *...  12.7 us
    ppermute x10, starting transfers between devices, move(): lax.ppermute(block, 'pool', [(g, (g + v) % group_count) for g in range(gr...  8.86 us
    pallas_call x1, Pallas kernels, project(): pl.pallas_call(project_kernel, out_shape=(pltpu.VMEM(out_shape, BF16), ja...  3.99 us
    unnamed x26, local copies, waits for them, and re-layouts  1.6 us
    pallas_call x1, Pallas kernels, plan(): pl.pallas_call(functools.partial(plan_kernel, low, capacity, group_count,...  1.59 us
    ppermute x1, waiting for transfers between devices, body(): other_sides = lax.ppermute(send_sides, 'dap', swap)  1.49 us
    slice x1, local copies, waits for them, and re-layouts, body(): picks += [choices[2 + k] for k in range(most - AT_ONCE)]  1.46 us
  transfers between devices with their start and end apart: 13, of which 8 were waited for; matrix products, arithmetic and copies ran while one was open for 2% of the time, Pallas kernels for 9%

profile of v3, /device:TPU:15, one launch (start us, length us, event | category | flops | bytes accessed | tf_op | source)
XLA Modules:
  0.0 63.6 jit_solution(4673749052732160452)
XLA Ops:
  0.0 0.7 %collective-permute-start.169 = (bf16[22,8,16,128]{3,2,1,0:T(8,128)(2,1)}, bf16[22,8,16,128]{3,2,1,0:T(8,128)(2,1)S(1)}, u32[]{:S(2)}, u32[]{:S(2)}) collective-permute-start(bf16[22,8,16,128]{3,2,1,0:T(8,128)(2,1)} %pair.1), channel_id=1, source_target_pairs={{0,1},{1,0},{2,3},{3,2},{4,5},{5,4},{6,7},{7,6},{8,9},{9,8},{10,11... | collective-permute-start | bytes 2162696 | tf_op jit(solution)/shard_map/ppermute | solution.py:660
  0.7 4.0 %project.1 = (bf16[11,32,256]{2,1,0:T(8,128)(2,1)S(1)}, bf16[11,32,256]{2,1,0:T(8,128)(2,1)}) custom-call(s32[176]{0:T(256)} %lengths_ref.1, bf16[22,16,8,256]{3,2,1,0:T(8,128)(2,1)} %alignment_in.1, bf16[64,256]{1,0:T(8,128)(2,1)} %bitcast.11, bf16[512,512]{1,0:T(8,128)(2,1)} %constant.15.clone.w_spread_in), custom_call_target="tpu_custom_call" | custom-call | flops 2000000000 | bytes 4000000 | tf_op jit(solution)/shard_map/project/pallas_call | solution.py:150
  4.9 1.5 %collective-permute-done.168.other_sides = bf16[11,32,256]{2,1,0:T(8,128)(2,1)S(1)} collective-permute-done((bf16[11,32,256]{2,1,0:T(8,128)(2,1)}, bf16[11,32,256]{2,1,0:T(8,128)(2,1)S(1)}, u32[]{:S(2)}, u32[]{:S(2)}) %collective-permute-start.168) | collective-permute-done | bytes 180256 | tf_op jit(solution)/shard_map/ppermute | solution.py:663
  6.5 0.9 %copy-done.4 = bf16[128,512]{1,0:T(8,128)(2,1)S(1)} copy-done((bf16[128,512]{1,0:T(8,128)(2,1)S(1)}, bf16[128,512]{1,0:T(8,128)(2,1)}, u32[]{:S(2)}) %copy-start.4) | copy-done | bytes 131096
  7.4 12.7 %pair_update.1 = (bf16[11,8,16,128]{3,2,1,0:T(8,128)(2,1)S(1)}, bf16[11,8,16,128]{3,2,1,0:T(8,128)(2,1)S(1)}) custom-call(s32[176]{0:T(256)S(1)} %copy-done.9, s32[176]{0:T(256)S(1)} %copy-done.10, bf16[11,32,256]{2,1,0:T(8,128)(2,1)S(1)} %get-tuple-element.654.own_sides, bf16[11,32,256]{2,1,0:T(8,128)(2,1)S(1)} %collective-permute-done.168.other_sides, ...), custom_call_target="tpu_custom_call" | custom-call | flops 10000000000 | bytes 4000000 | tf_op jit(solution)/shard_map/pair_update/pallas_call | solution.py:378
  20.3 1.6 %plan.1.plan_ref = s32[65]{0:T(128)} custom-call(s32[22]{0:T(128)} %shifts_ref.1), custom_call_target="tpu_custom_call" | custom-call | flops 1000000 | bytes 1000000 | tf_op jit(solution)/shard_map/plan/pallas_call | solution.py:561
  21.9 1.5 %fusion = (s32[1]{0:T(128)}, s32[1]{0:T(128)}, s32[1]{0:T(128)}, s32[1]{0:T(128)}) fusion(s32[65]{0:T(128)} %plan.1.plan_ref), kind=kLoop, calls=%fused_computation | loop fusion | bytes 32 | tf_op jit(solution)/shard_map/slice | solution.py:674
  24.1 0.6 %copy-done = s32[65]{0:T(128)S(1)} copy-done((s32[65]{0:T(128)S(1)}, s32[65]{0:T(128)}, u32[]{:S(2)}) %copy-start) | copy-done | bytes 284
  24.7 0.9 %pack.1 = (bf16[3,8,16,128]{3,2,1,0:T(8,128)(2,1)S(1)}, bf16[3,8,16,128]{3,2,1,0:T(8,128)(2,1)S(1)}, bf16[3,8,16,128]{3,2,1,0:T(8,128)(2,1)S(1)}, bf16[3,8,16,12...) custom-call(s32[65]{0:T(128)S(1)} %copy-done, ...), custom_call_target="tpu_custom_call" | custom-call | tf_op jit(solution)/shard_map/pack/pallas_call | solution.py:580
  25.7 1.3 %collective-permute-start.171 = (bf16[3,8,16,128]{3,2,1,0:T(8,128)(2,1)S(1)}, bf16[3,8,16,128]{3,2,1,0:T(8,128)(2,1)S(1)}, u32[]{:S(2)}, u32[]{:S(2)}) collective-permute-start(bf16[3,8,16,128]{3,2,1,0:T(8,128)(2,1)S(1)} %get-tuple-element.659), channel_id=1, source_target_pairs={{0,2},{2,4},{4,6},{6,8},{8,10},{10,12},{12,14},{14,0},{1,3},{3,5},... | collective-permute-start | bytes 294920 | tf_op jit(solution)/shard_map/ppermute | solution.py:592
  27.0 1.3 %collective-permute-start.172 = (bf16[3,8,16,128]{3,2,1,0:T(8,128)(2,1)S(1)}, bf16[3,8,16,128]{3,2,1,0:T(8,128)(2,1)S(1)}, u32[]{:S(2)}, u32[]{:S(2)}) collective-permute-start(bf16[3,8,16,128]{3,2,1,0:T(8,128)(2,1)S(1)} %get-tuple-element.660), channel_id=1, source_target_pairs={{0,4},{2,6},{4,8},{6,10},{8,12},{10,14},{12,0},{14,2},{1,5},{3,7},... | collective-permute-start | bytes 294920 | tf_op jit(solution)/shard_map/ppermute | solution.py:592
  28.9 15.0 %conditional.4 = ((bf16[3,8,16,128]{3,2,1,0:T(8,128)(2,1)S(1)}, bf16[3,8,16,128]{3,2,1,0:T(8,128)(2,1)S(1)}, bf16[3,8,16,128]{3,2,1,0:T(8,128)(2,1)S(1)})) conditional(s32[]{:T(128)} %clamp.12, (bf16[3,8,16,128]{3,2,1,0:T(8,128)(2,1)S(1)}, bf16[3,8,16,128]{3,2,1,0:T(8,128)(2,1)S(1)}, ...), branch_computations={%region_0.0_spmd, %region_1.0_spmd, %region_2.0_spmd, %region_3.0_... | conditional | bytes 1769624 | solution.py:607
  29.2 1.0 %collective-permute-start.127 = (bf16[3,8,16,128]{3,2,1,0:T(8,128)(2,1)S(1)}, bf16[3,8,16,128]{3,2,1,0:T(8,128)(2,1)S(1)}, u32[]{:S(2)}, u32[]{:S(2)}) collective-permute-start(bf16[3,8,16,128]{3,2,1,0:T(8,128)(2,1)S(1)} %get-tuple-element.597), channel_id=1, source_target_pairs={{0,6},{2,8},{4,10},{6,12},{8,14},{10,0},{12,2},{14,4},{1,7},{3,9},... | collective-permute-start | bytes 294920 | tf_op jit(solution)/shard_map/cond/branch_55_fun/ppermute | solution.py:592
  30.2 1.3 %collective-permute-start.128 = (bf16[3,8,16,128]{3,2,1,0:T(8,128)(2,1)S(1)}, bf16[3,8,16,128]{3,2,1,0:T(8,128)(2,1)S(1)}, u32[]{:S(2)}, u32[]{:S(2)}) collective-permute-start(bf16[3,8,16,128]{3,2,1,0:T(8,128)(2,1)S(1)} %get-tuple-element.598), channel_id=1, source_target_pairs={{0,8},{2,10},{4,12},{6,14},{8,0},{10,2},{12,4},{14,6},{1,9},{3,11}... | collective-permute-start | bytes 294920 | tf_op jit(solution)/shard_map/cond/branch_55_fun/ppermute | solution.py:592
  31.7 7.6 %collective-permute-done.127 = bf16[3,8,16,128]{3,2,1,0:T(8,128)(2,1)S(1)} collective-permute-done((bf16[3,8,16,128]{3,2,1,0:T(8,128)(2,1)S(1)}, bf16[3,8,16,128]{3,2,1,0:T(8,128)(2,1)S(1)}, u32[]{:S(2)}, u32[]{:S(2)}) %collective-permute-start.127) | collective-permute-done | bytes 98336 | tf_op jit(solution)/shard_map/cond/branch_55_fun/ppermute | solution.py:592
  39.3 2.1 %collective-permute-done.128 = bf16[3,8,16,128]{3,2,1,0:T(8,128)(2,1)S(1)} collective-permute-done((bf16[3,8,16,128]{3,2,1,0:T(8,128)(2,1)S(1)}, bf16[3,8,16,128]{3,2,1,0:T(8,128)(2,1)S(1)}, u32[]{:S(2)}, u32[]{:S(2)}) %collective-permute-start.128) | collective-permute-done | bytes 98336 | tf_op jit(solution)/shard_map/cond/branch_55_fun/ppermute | solution.py:592
  41.4 2.5 %collective-permute-done.129 = bf16[3,8,16,128]{3,2,1,0:T(8,128)(2,1)S(1)} collective-permute-done((bf16[3,8,16,128]{3,2,1,0:T(8,128)(2,1)S(1)}, bf16[3,8,16,128]{3,2,1,0:T(8,128)(2,1)S(1)}, u32[]{:S(2)}, u32[]{:S(2)}) %collective-permute-start.129) | collective-permute-done | bytes 98336 | tf_op jit(solution)/shard_map/cond/branch_55_fun/ppermute | solution.py:592
  44.0 0.7 %collective-permute-start.174 = (bf16[3,8,16,128]{3,2,1,0:T(8,128)(2,1)S(1)}, bf16[3,8,16,128]{3,2,1,0:T(8,128)(2,1)S(1)}, u32[]{:S(2)}, u32[]{:S(2)}) collective-permute-start(bf16[3,8,16,128]{3,2,1,0:T(8,128)(2,1)S(1)} %get-tuple-element.662), channel_id=1, source_target_pairs={{0,8},{2,10},{4,12},{6,14},{8,0},{10,2},{12,4},{14,6},{1,9},{3,11}... | collective-permute-start | bytes 294920 | tf_op jit(solution)/shard_map/ppermute | solution.py:592
  44.7 2.3 %collective-permute-start.175 = (bf16[3,8,16,128]{3,2,1,0:T(8,128)(2,1)S(1)}, bf16[3,8,16,128]{3,2,1,0:T(8,128)(2,1)S(1)}, u32[]{:S(2)}, u32[]{:S(2)}) collective-permute-start(bf16[3,8,16,128]{3,2,1,0:T(8,128)(2,1)S(1)} %get-tuple-element.663), channel_id=1, source_target_pairs={{0,10},{2,12},{4,14},{6,0},{8,2},{10,4},{12,6},{14,8},{1,11},{3,13... | collective-permute-start | bytes 294920 | tf_op jit(solution)/shard_map/ppermute | solution.py:592
  47.0 0.7 %collective-permute-start.176 = (bf16[3,8,16,128]{3,2,1,0:T(8,128)(2,1)S(1)}, bf16[3,8,16,128]{3,2,1,0:T(8,128)(2,1)S(1)}, u32[]{:S(2)}, u32[]{:S(2)}) collective-permute-start(bf16[3,8,16,128]{3,2,1,0:T(8,128)(2,1)S(1)} %get-tuple-element.664), channel_id=1, source_target_pairs={{0,12},{2,14},{4,0},{6,2},{8,4},{10,6},{12,8},{14,10},{1,13},{3,15... | collective-permute-start | bytes 294920 | tf_op jit(solution)/shard_map/ppermute | solution.py:592
  47.7 5.9 %collective-permute-done.173.refs_2_ = bf16[3,8,16,128]{3,2,1,0:T(8,128)(2,1)S(1)} collective-permute-done((bf16[3,8,16,128]{3,2,1,0:T(8,128)(2,1)S(1)}, bf16[3,8,16,128]{3,2,1,0:T(8,128)(2,1)S(1)}, u32[]{:S(2)}, u32[]{:S(2)}) %collective-permute-start.173) | collective-permute-done | bytes 98336 | tf_op jit(solution)/shard_map/ppermute | solution.py:592
  53.6 2.2 %collective-permute-done.174.refs_3_ = bf16[3,8,16,128]{3,2,1,0:T(8,128)(2,1)S(1)} collective-permute-done((bf16[3,8,16,128]{3,2,1,0:T(8,128)(2,1)S(1)}, bf16[3,8,16,128]{3,2,1,0:T(8,128)(2,1)S(1)}, u32[]{:S(2)}, u32[]{:S(2)}) %collective-permute-start.174) | collective-permute-done | bytes 98336 | tf_op jit(solution)/shard_map/ppermute | solution.py:592
  56.3 5.8 %collective-permute-done.177.refs_6_ = bf16[3,8,16,128]{3,2,1,0:T(8,128)(2,1)S(1)} collective-permute-done((bf16[3,8,16,128]{3,2,1,0:T(8,128)(2,1)S(1)}, bf16[3,8,16,128]{3,2,1,0:T(8,128)(2,1)S(1)}, u32[]{:S(2)}, u32[]{:S(2)}) %collective-permute-start.177) | collective-permute-done | bytes 98336 | tf_op jit(solution)/shard_map/ppermute | solution.py:592
  62.0 1.4 %unpack.1 = bf16[22,8,16,128]{3,2,1,0:T(8,128)(2,1)} custom-call(s32[65]{0:T(128)S(1)} %copy-done.1, bf16[11,8,16,128]{3,2,1,0:T(8,128)(2,1)S(1)} %get-tuple-element.656.keep, bf16[11,8,16,128]{3,2,1,0:T(8,128)(2,1)S(1)} %collective-permute-done.170.other, bf16[3,8,16,128]{3,2,1,0:T(8,128)(2,1)S(1)} %collective-permute-done.171.refs_0_, ...), custom_call_target="tpu_custom_call" | custom-call | tf_op jit(solution)/shard_map/unpack/pallas_call | solution.py:618
  (40 shorter events, 1.1 us)
Async XLA Ops:
  0.0 6.4 %collective-permute-start.169 = (bf16[22,8,16,128]{3,2,1,0:T(8,128)(2,1)}, bf16[22,8,16,128]{3,2,1,0:T(8,128)(2,1)S(1)}, u32[]{:S(2)}, u32[]{:S(2)}) collective-permute-start(bf16[22,8,16,128]{3,2,1,0:T(8,128)(2,1)} %pair.1), channel_id=1, source_target_pairs={{0,1},{1,0},{2,3},{3,2},{4,5},{5,4},{6,7},{7,6},{8,9},{9,8},{10,11... | collective-permute-start | bytes 2162696 | tf_op jit(solution)/shard_map/ppermute | solution.py:660
  0.7 4.2 %copy-start.12 = (bf16[1024,128]{1,0:T(8,128)(2,1)S(1)}, bf16[1024,128]{1,0:T(8,128)(2,1)}, u32[]{:S(2)}) copy-start(bf16[1024,128]{1,0:T(8,128)(2,1)} %param.103) | copy-start | bytes 786436
  0.7 5.8 %copy-start.2 = (bf16[22,8,16,128]{3,2,1,0:T(8,128)(2,1)S(1)}, bf16[22,8,16,128]{3,2,1,0:T(8,128)(2,1)}, u32[]{:S(2)}) copy-start(bf16[22,8,16,128]{3,2,1,0:T(8,128)(2,1)} %pair.1) | copy-start | bytes 2162692
  0.7 5.8 %copy-start.3 = (bf16[128,512]{1,0:T(8,128)(2,1)S(1)}, bf16[128,512]{1,0:T(8,128)(2,1)}, u32[]{:S(2)}) copy-start(bf16[128,512]{1,0:T(8,128)(2,1)} %out_ab.1) | copy-start | bytes 393220
  0.7 5.8 %copy-start.5 = (bf16[128,128]{1,0:T(8,128)(2,1)S(1)}, bf16[128,128]{1,0:T(8,128)(2,1)}, u32[]{:S(2)}) copy-start(bf16[128,128]{1,0:T(8,128)(2,1)} %out_gate.1) | copy-start | bytes 98308
  0.7 5.8 %copy-start.6 = (bf16[128,128]{1,0:T(8,128)(2,1)S(1)}, bf16[128,128]{1,0:T(8,128)(2,1)}, u32[]{:S(2)}) copy-start(bf16[128,128]{1,0:T(8,128)(2,1)} %out_proj.1) | copy-start | bytes 98308
  0.7 5.8 %copy-start.7 = (bf16[128,128]{1,0:T(8,128)(2,1)S(1)}, bf16[128,128]{1,0:T(8,128)(2,1)}, u32[]{:S(2)}) copy-start(bf16[128,128]{1,0:T(8,128)(2,1)} %in_gate.1) | copy-start | bytes 98308
  0.7 5.8 %copy-start.8 = (bf16[128,128]{1,0:T(8,128)(2,1)S(1)}, bf16[128,128]{1,0:T(8,128)(2,1)}, u32[]{:S(2)}) copy-start(bf16[128,128]{1,0:T(8,128)(2,1)} %in_proj.1) | copy-start | bytes 98308
  0.7 5.8 %copy-start.9 = (s32[176]{0:T(256)S(1)}, s32[176]{0:T(256)}, u32[]{:S(2)}) copy-start(s32[176]{0:T(256)} %lengths_ref.1) | copy-start | bytes 2116
  0.7 5.8 %copy-start.10 = (s32[176]{0:T(256)S(1)}, s32[176]{0:T(256)}, u32[]{:S(2)}) copy-start(s32[176]{0:T(256)} %breaks_ref.1) | copy-start | bytes 2116
  0.7 5.8 %copy-start.11 = (bf16[2,128]{1,0:T(2,128)(2,1)S(1)}, bf16[2,128]{1,0:T(2,128)(2,1)}, u32[]{:S(2)}) copy-start(bf16[2,128]{1,0:T(2,128)(2,1)} %bias.1) | copy-start | bytes 1540
  4.7 1.7 %collective-permute-start.168 = (bf16[11,32,256]{2,1,0:T(8,128)(2,1)}, bf16[11,32,256]{2,1,0:T(8,128)(2,1)S(1)}, u32[]{:S(2)}, u32[]{:S(2)}) collective-permute-start(bf16[11,32,256]{2,1,0:T(8,128)(2,1)} %get-tuple-element.655), channel_id=1, source_target_pairs={{0,1},{1,0},{2,3},{3,2},{4,5},{5,4},{6,7},{7,6},{8,9},{9,8},{10,11... | collective-permute-start | bytes 540680 | tf_op jit(solution)/shard_map/ppermute | solution.py:663
  20.1 3.9 %collective-permute-start.170 = (bf16[11,8,16,128]{3,2,1,0:T(8,128)(2,1)S(1)}, bf16[11,8,16,128]{3,2,1,0:T(8,128)(2,1)S(1)}, u32[]{:S(2)}, u32[]{:S(2)}) collective-permute-start(bf16[11,8,16,128]{3,2,1,0:T(8,128)(2,1)S(1)} %get-tuple-element.657), channel_id=1, source_target_pairs={{0,1},{1,0},{2,3},{3,2},{4,5},{5,4},{6,7},{7,6},{8,9},{9,8},{10,11... | collective-permute-start | bytes 1081352 | tf_op jit(solution)/shard_map/ppermute | solution.py:670
  25.7 21.3 %collective-permute-start.171 = (bf16[3,8,16,128]{3,2,1,0:T(8,128)(2,1)S(1)}, bf16[3,8,16,128]{3,2,1,0:T(8,128)(2,1)S(1)}, u32[]{:S(2)}, u32[]{:S(2)}) collective-permute-start(bf16[3,8,16,128]{3,2,1,0:T(8,128)(2,1)S(1)} %get-tuple-element.659), channel_id=1, source_target_pairs={{0,2},{2,4},{4,6},{6,8},{8,10},{10,12},{12,14},{14,0},{1,3},{3,5},... | collective-permute-start | bytes 294920 | tf_op jit(solution)/shard_map/ppermute | solution.py:592
  27.0 20.8 %collective-permute-start.172 = (bf16[3,8,16,128]{3,2,1,0:T(8,128)(2,1)S(1)}, bf16[3,8,16,128]{3,2,1,0:T(8,128)(2,1)S(1)}, u32[]{:S(2)}, u32[]{:S(2)}) collective-permute-start(bf16[3,8,16,128]{3,2,1,0:T(8,128)(2,1)S(1)} %get-tuple-element.660), channel_id=1, source_target_pairs={{0,4},{2,6},{4,8},{6,10},{8,12},{10,14},{12,0},{14,2},{1,5},{3,7},... | collective-permute-start | bytes 294920 | tf_op jit(solution)/shard_map/ppermute | solution.py:592
  29.2 10.1 %collective-permute-start.127 = (bf16[3,8,16,128]{3,2,1,0:T(8,128)(2,1)S(1)}, bf16[3,8,16,128]{3,2,1,0:T(8,128)(2,1)S(1)}, u32[]{:S(2)}, u32[]{:S(2)}) collective-permute-start(bf16[3,8,16,128]{3,2,1,0:T(8,128)(2,1)S(1)} %get-tuple-element.597), channel_id=1, source_target_pairs={{0,6},{2,8},{4,10},{6,12},{8,14},{10,0},{12,2},{14,4},{1,7},{3,9},... | collective-permute-start | bytes 294920 | tf_op jit(solution)/shard_map/cond/branch_55_fun/ppermute | solution.py:592
  30.2 11.2 %collective-permute-start.128 = (bf16[3,8,16,128]{3,2,1,0:T(8,128)(2,1)S(1)}, bf16[3,8,16,128]{3,2,1,0:T(8,128)(2,1)S(1)}, u32[]{:S(2)}, u32[]{:S(2)}) collective-permute-start(bf16[3,8,16,128]{3,2,1,0:T(8,128)(2,1)S(1)} %get-tuple-element.598), channel_id=1, source_target_pairs={{0,8},{2,10},{4,12},{6,14},{8,0},{10,2},{12,4},{14,6},{1,9},{3,11}... | collective-permute-start | bytes 294920 | tf_op jit(solution)/shard_map/cond/branch_55_fun/ppermute | solution.py:592
  31.6 12.4 %collective-permute-start.129 = (bf16[3,8,16,128]{3,2,1,0:T(8,128)(2,1)S(1)}, bf16[3,8,16,128]{3,2,1,0:T(8,128)(2,1)S(1)}, u32[]{:S(2)}, u32[]{:S(2)}) collective-permute-start(bf16[3,8,16,128]{3,2,1,0:T(8,128)(2,1)S(1)} %get-tuple-element.599), channel_id=1, source_target_pairs={{0,12},{2,14},{4,0},{6,2},{8,4},{10,6},{12,8},{14,10},{1,13},{3,15... | collective-permute-start | bytes 294920 | tf_op jit(solution)/shard_map/cond/branch_55_fun/ppermute | solution.py:592
  44.0 18.1 %copy-start.1 = (s32[65]{0:T(128)S(1)}, s32[65]{0:T(128)}, u32[]{:S(2)}) copy-start(s32[65]{0:T(128)} %plan.1.plan_ref) | copy-start | bytes 784
  44.0 9.7 %collective-permute-start.173 = (bf16[3,8,16,128]{3,2,1,0:T(8,128)(2,1)S(1)}, bf16[3,8,16,128]{3,2,1,0:T(8,128)(2,1)S(1)}, u32[]{:S(2)}, u32[]{:S(2)}) collective-permute-start(bf16[3,8,16,128]{3,2,1,0:T(8,128)(2,1)S(1)} %get-tuple-element.661), channel_id=1, source_target_pairs={{0,6},{2,8},{4,10},{6,12},{8,14},{10,0},{12,2},{14,4},{1,7},{3,9},... | collective-permute-start | bytes 294920 | tf_op jit(solution)/shard_map/ppermute | solution.py:592
  44.0 11.9 %collective-permute-start.174 = (bf16[3,8,16,128]{3,2,1,0:T(8,128)(2,1)S(1)}, bf16[3,8,16,128]{3,2,1,0:T(8,128)(2,1)S(1)}, u32[]{:S(2)}, u32[]{:S(2)}) collective-permute-start(bf16[3,8,16,128]{3,2,1,0:T(8,128)(2,1)S(1)} %get-tuple-element.662), channel_id=1, source_target_pairs={{0,8},{2,10},{4,12},{6,14},{8,0},{10,2},{12,4},{14,6},{1,9},{3,11}... | collective-permute-start | bytes 294920 | tf_op jit(solution)/shard_map/ppermute | solution.py:592
  44.7 11.2 %collective-permute-start.175 = (bf16[3,8,16,128]{3,2,1,0:T(8,128)(2,1)S(1)}, bf16[3,8,16,128]{3,2,1,0:T(8,128)(2,1)S(1)}, u32[]{:S(2)}, u32[]{:S(2)}) collective-permute-start(bf16[3,8,16,128]{3,2,1,0:T(8,128)(2,1)S(1)} %get-tuple-element.663), channel_id=1, source_target_pairs={{0,10},{2,12},{4,14},{6,0},{8,2},{10,4},{12,6},{14,8},{1,11},{3,13... | collective-permute-start | bytes 294920 | tf_op jit(solution)/shard_map/ppermute | solution.py:592
  47.0 9.3 %collective-permute-start.176 = (bf16[3,8,16,128]{3,2,1,0:T(8,128)(2,1)S(1)}, bf16[3,8,16,128]{3,2,1,0:T(8,128)(2,1)S(1)}, u32[]{:S(2)}, u32[]{:S(2)}) collective-permute-start(bf16[3,8,16,128]{3,2,1,0:T(8,128)(2,1)S(1)} %get-tuple-element.664), channel_id=1, source_target_pairs={{0,12},{2,14},{4,0},{6,2},{8,4},{10,6},{12,8},{14,10},{1,13},{3,15... | collective-permute-start | bytes 294920 | tf_op jit(solution)/shard_map/ppermute | solution.py:592
  47.7 14.3 %collective-permute-start.177 = (bf16[3,8,16,128]{3,2,1,0:T(8,128)(2,1)S(1)}, bf16[3,8,16,128]{3,2,1,0:T(8,128)(2,1)S(1)}, u32[]{:S(2)}, u32[]{:S(2)}) collective-permute-start(bf16[3,8,16,128]{3,2,1,0:T(8,128)(2,1)S(1)} %get-tuple-element.665), channel_id=1, source_target_pairs={{0,14},{2,0},{4,2},{6,4},{8,6},{10,8},{12,10},{14,12},{1,15},{3,1}... | collective-permute-start | bytes 294920 | tf_op jit(solution)/shard_map/ppermute | solution.py:592
  (2 other events, 1.6 us)

commit v4 on v3

--- a/solution.py
+++ b/solution.py
@@ -71,10 +71,17 @@
     half = lax.axis_index("dap")
     mine, theirs = half * count, (1 - half) * count
     home = lax.axis_index("pool") * slots
+    ways = side.shape[0] // 2
+    pieces_in = [
+        (alignment_in.at[pl.ds(start + first, size)], alignment.at[pl.ds(start + first, size)])
+        for first, size in ((0, ways), (ways, count - ways))
+        for start in (mine, theirs)
+        if size > 0
+    ]
     copies = [
         pltpu.make_async_copy(source, target, sems.at[n])
         for n, (source, target) in enumerate(
-            ((w_align_in, w_align), (lengths_in, lengths_ref), (alignment_in, alignment), (w_spread_in, w_spread))
+            [(w_align_in, w_align), (lengths_in, lengths_ref)] + pieces_in + [(w_spread_in, w_spread)]
         )
     ]
     for copy in copies:
@@ -88,8 +95,8 @@
         w_align[...], repeat, (((0,), (0,)), ((), ())), preferred_element_type=F32
     ).astype(BF16)
     residue = lax.broadcasted_iota(jnp.int32, (rows, 1), 0) + half * rows
-    copies[1].wait()
-    copies[2].wait()
+    for copy in copies[1:4]:
+        copy.wait()
 
     def one(index, start, which, way, out_ref):
         length = lengths_ref[home + start + index]
@@ -101,7 +108,7 @@
         values = dot((values * lax.rsqrt(spread + EPSILON)).astype(BF16), w_project)
         yield
         values = values.reshape(depth, rows, 2 * LANES) * jnp.where(residue < length, 1.0, 0.0)
-        side[way] = values[:, :, :LANES].reshape(depth * rows, LANES) * (1.0 / depth)
+        side[way, : depth * rows] = values[:, :, :LANES].reshape(depth * rows, LANES) * (1.0 / depth)
         tiles = []
         for tile in range(rows // pieces):
             piece = side[way, pl.ds(tile * pieces, depth, stride=rows), :]
@@ -116,9 +123,12 @@
                 piece = jnp.where(groups[q], values[tile * pieces + q, :, LANES:], piece)
             rights[which, index, :, LANES * tile : LANES * tile + LANES] = piece
 
-    ways = side.shape[0] // 2
-
     def step(round_, carry):
+        @pl.when(round_ == 1)
+        def _():
+            for copy in copies[4:-1]:
+                copy.wait()
+
         streams = []
         for way in range(ways):
             index = jnp.minimum(round_ * ways + way, count - 1)
@@ -128,7 +138,7 @@
         return carry
 
     lax.fori_loop(0, (count + ways - 1) // ways, step, 0)
-    copies[3].wait()
+    copies[-1].wait()
     flat = rights[...].reshape(slots * rows, depth * inner).astype(BF16)
     spread = dot(flat, w_spread[...]).reshape(2, count, rows, depth * inner).astype(BF16)
     parts = own_ref.shape[-1]
@@ -157,9 +167,9 @@
             pltpu.VMEM(alignment.shape, BF16),
             pltpu.VMEM(w_align.shape, BF16),
             pltpu.VMEM(w_spread.shape, BF16),
-            pltpu.VMEM((2 * PROJECT_WAYS, depth * rows, LANES), F32),
+            pltpu.VMEM((2 * PROJECT_WAYS, depth * rows + rows, LANES), F32),
             pltpu.VMEM((2, count, rows, depth * inner), F32),
-            pltpu.SemaphoreType.DMA((4,)),
+            pltpu.SemaphoreType.DMA((7,)),
         ],
         compiler_params=pltpu.CompilerParams(vmem_limit_bytes=PROJECT_LIMIT),
         cost_estimate=pl.CostEstimate(flops=2 * 10**9, bytes_accessed=4 * 10**6, transcendentals=0),
@@ -280,7 +290,7 @@
         yield
         for n in range(2):
             projected = dot(x, w_ab[:, 2 * hidden * n : 2 * hidden * n + 2 * hidden])
-            sides_refs[way, first + n] = (jnp.tanh(projected[:, hidden:]) + 1.0) * projected[:, :hidden]
+            sides_refs[way, first + n, :pairs] = (jnp.tanh(projected[:, hidden:]) + 1.0) * projected[:, :hidden]
             yield
         gates_refs[way] = jnp.tanh(dot(x, w_gate[...])) + 1.0
 
@@ -385,7 +395,7 @@
             pltpu.VMEM((WAYS, pairs, width), F32),
             pltpu.VMEM((WAYS, pairs, width), F32),
             pltpu.VMEM((WAYS, pairs, width), F32),
-            pltpu.VMEM((WAYS, 4, pairs, hidden), F32),
+            pltpu.VMEM((WAYS, 4, pairs + full, hidden), F32),
         ],
         compiler_params=pltpu.CompilerParams(vmem_limit_bytes=VMEM_LIMIT),
         cost_estimate=pl.CostEstimate(flops=10**10, bytes_accessed=4 * 10**6, transcendentals=0),

time: 63.8 us -> 63.6 us (level)
  transfers between devices with their start and end apart: 13 -> 13, of which waited for: 8 -> 8; matrix products, arithmetic and copies ran while one was open for 2% -> 3% of each run, Pallas kernels for 9% -> 8%
where the time goes in v4:
time: 63.6 us; the launch traced here: 63.4 us
  waiting for transfers between devices  28 us (44%)
  Pallas kernels  20.4 us (32%)
  starting transfers between devices  9.82 us (15%)
  local copies, waits for them, and re-layouts  3.19 us (5%)
  between operations  1.67 us (3%)
    ppermute x10, waiting for transfers between devices, move(): lax.ppermute(block, 'pool', [(g, (g + v) % group_count) for g in range(gr...  26.5 us
    pallas_call x1, Pallas kernels, update(): pl.pallas_call(update_kernel, out_shape=(shape, shape), in_specs=[smem] *...  12.7 us
    ppermute x10, starting transfers between devices, move(): lax.ppermute(block, 'pool', [(g, (g + v) % group_count) for g in range(gr...  8.86 us
    pallas_call x1, Pallas kernels, project(): pl.pallas_call(project_kernel, out_shape=(pltpu.VMEM(out_shape, BF16), ja...  3.78 us
    unnamed x26, local copies, waits for them, and re-layouts  1.6 us
    pallas_call x1, Pallas kernels, plan(): pl.pallas_call(functools.partial(plan_kernel, low, capacity, group_count,...  1.59 us
    ppermute x1, waiting for transfers between devices, body(): other_sides = lax.ppermute(send_sides, 'dap', swap)  1.49 us
    slice x1, local copies, waits for them, and re-layouts, body(): picks += [choices[2 + k] for k in range(most - AT_ONCE)]  1.46 us
  transfers between devices with their start and end apart: 13, of which 8 were waited for; matrix products, arithmetic and copies ran while one was open for 3% of the time, Pallas kernels for 8%

profile of v4, /device:TPU:15, one launch (start us, length us, event | category | flops | bytes accessed | tf_op | source)
XLA Modules:
  0.0 63.4 jit_solution(17079449782232799610)
XLA Ops:
  0.0 0.7 %collective-permute-start.169 = (bf16[22,8,16,128]{3,2,1,0:T(8,128)(2,1)}, bf16[22,8,16,128]{3,2,1,0:T(8,128)(2,1)S(1)}, u32[]{:S(2)}, u32[]{:S(2)}) collective-permute-start(bf16[22,8,16,128]{3,2,1,0:T(8,128)(2,1)} %pair.1), channel_id=1, source_target_pairs={{0,1},{1,0},{2,3},{3,2},{4,5},{5,4},{6,7},{7,6},{8,9},{9,8},{10,11... | collective-permute-start | bytes 2162696 | tf_op jit(solution)/shard_map/ppermute | solution.py:670
  0.7 3.8 %project.1 = (bf16[11,32,256]{2,1,0:T(8,128)(2,1)S(1)}, bf16[11,32,256]{2,1,0:T(8,128)(2,1)}) custom-call(s32[176]{0:T(256)} %lengths_ref.1, bf16[22,16,8,256]{3,2,1,0:T(8,128)(2,1)} %alignment_in.1, bf16[64,256]{1,0:T(8,128)(2,1)} %bitcast.11, bf16[512,512]{1,0:T(8,128)(2,1)} %constant.15.clone.w_spread_in), custom_call_target="tpu_custom_call" | custom-call | flops 2000000000 | bytes 4000000 | tf_op jit(solution)/shard_map/project/pallas_call | solution.py:160
  4.7 1.5 %collective-permute-done.168.other_sides = bf16[11,32,256]{2,1,0:T(8,128)(2,1)S(1)} collective-permute-done((bf16[11,32,256]{2,1,0:T(8,128)(2,1)}, bf16[11,32,256]{2,1,0:T(8,128)(2,1)S(1)}, u32[]{:S(2)}, u32[]{:S(2)}) %collective-permute-start.168) | collective-permute-done | bytes 180256 | tf_op jit(solution)/shard_map/ppermute | solution.py:673
  6.3 0.9 %copy-done.4 = bf16[128,512]{1,0:T(8,128)(2,1)S(1)} copy-done((bf16[128,512]{1,0:T(8,128)(2,1)S(1)}, bf16[128,512]{1,0:T(8,128)(2,1)}, u32[]{:S(2)}) %copy-start.4) | copy-done | bytes 131096
  7.2 12.7 %pair_update.1 = (bf16[11,8,16,128]{3,2,1,0:T(8,128)(2,1)S(1)}, bf16[11,8,16,128]{3,2,1,0:T(8,128)(2,1)S(1)}) custom-call(s32[176]{0:T(256)S(1)} %copy-done.9, s32[176]{0:T(256)S(1)} %copy-done.10, bf16[11,32,256]{2,1,0:T(8,128)(2,1)S(1)} %get-tuple-element.654.own_sides, bf16[11,32,256]{2,1,0:T(8,128)(2,1)S(1)} %collective-permute-done.168.other_sides, ...), custom_call_target="tpu_custom_call" | custom-call | flops 10000000000 | bytes 4000000 | tf_op jit(solution)/shard_map/pair_update/pallas_call | solution.py:388
  20.1 1.6 %plan.1.plan_ref = s32[65]{0:T(128)} custom-call(s32[22]{0:T(128)} %shifts_ref.1), custom_call_target="tpu_custom_call" | custom-call | flops 1000000 | bytes 1000000 | tf_op jit(solution)/shard_map/plan/pallas_call | solution.py:571
  21.7 1.5 %fusion = (s32[1]{0:T(128)}, s32[1]{0:T(128)}, s32[1]{0:T(128)}, s32[1]{0:T(128)}) fusion(s32[65]{0:T(128)} %plan.1.plan_ref), kind=kLoop, calls=%fused_computation | loop fusion | bytes 32 | tf_op jit(solution)/shard_map/slice | solution.py:684
  23.9 0.6 %copy-done = s32[65]{0:T(128)S(1)} copy-done((s32[65]{0:T(128)S(1)}, s32[65]{0:T(128)}, u32[]{:S(2)}) %copy-start) | copy-done | bytes 284
  24.5 0.9 %pack.1 = (bf16[3,8,16,128]{3,2,1,0:T(8,128)(2,1)S(1)}, bf16[3,8,16,128]{3,2,1,0:T(8,128)(2,1)S(1)}, bf16[3,8,16,128]{3,2,1,0:T(8,128)(2,1)S(1)}, bf16[3,8,16,12...) custom-call(s32[65]{0:T(128)S(1)} %copy-done, ...), custom_call_target="tpu_custom_call" | custom-call | tf_op jit(solution)/shard_map/pack/pallas_call | solution.py:590
  25.5 1.3 %collective-permute-start.171 = (bf16[3,8,16,128]{3,2,1,0:T(8,128)(2,1)S(1)}, bf16[3,8,16,128]{3,2,1,0:T(8,128)(2,1)S(1)}, u32[]{:S(2)}, u32[]{:S(2)}) collective-permute-start(bf16[3,8,16,128]{3,2,1,0:T(8,128)(2,1)S(1)} %get-tuple-element.659), channel_id=1, source_target_pairs={{0,2},{2,4},{4,6},{6,8},{8,10},{10,12},{12,14},{14,0},{1,3},{3,5},... | collective-permute-start | bytes 294920 | tf_op jit(solution)/shard_map/ppermute | solution.py:602
  26.8 1.3 %collective-permute-start.172 = (bf16[3,8,16,128]{3,2,1,0:T(8,128)(2,1)S(1)}, bf16[3,8,16,128]{3,2,1,0:T(8,128)(2,1)S(1)}, u32[]{:S(2)}, u32[]{:S(2)}) collective-permute-start(bf16[3,8,16,128]{3,2,1,0:T(8,128)(2,1)S(1)} %get-tuple-element.660), channel_id=1, source_target_pairs={{0,4},{2,6},{4,8},{6,10},{8,12},{10,14},{12,0},{14,2},{1,5},{3,7},... | collective-permute-start | bytes 294920 | tf_op jit(solution)/shard_map/ppermute | solution.py:602
  28.7 15.0 %conditional.4 = ((bf16[3,8,16,128]{3,2,1,0:T(8,128)(2,1)S(1)}, bf16[3,8,16,128]{3,2,1,0:T(8,128)(2,1)S(1)}, bf16[3,8,16,128]{3,2,1,0:T(8,128)(2,1)S(1)})) conditional(s32[]{:T(128)} %clamp.12, (bf16[3,8,16,128]{3,2,1,0:T(8,128)(2,1)S(1)}, bf16[3,8,16,128]{3,2,1,0:T(8,128)(2,1)S(1)}, ...), branch_computations={%region_0.0_spmd, %region_1.0_spmd, %region_2.0_spmd, %region_3.0_... | conditional | bytes 1769624 | solution.py:617
  29.0 1.0 %collective-permute-start.127 = (bf16[3,8,16,128]{3,2,1,0:T(8,128)(2,1)S(1)}, bf16[3,8,16,128]{3,2,1,0:T(8,128)(2,1)S(1)}, u32[]{:S(2)}, u32[]{:S(2)}) collective-permute-start(bf16[3,8,16,128]{3,2,1,0:T(8,128)(2,1)S(1)} %get-tuple-element.597), channel_id=1, source_target_pairs={{0,6},{2,8},{4,10},{6,12},{8,14},{10,0},{12,2},{14,4},{1,7},{3,9},... | collective-permute-start | bytes 294920 | tf_op jit(solution)/shard_map/cond/branch_55_fun/ppermute | solution.py:602
  30.0 1.3 %collective-permute-start.128 = (bf16[3,8,16,128]{3,2,1,0:T(8,128)(2,1)S(1)}, bf16[3,8,16,128]{3,2,1,0:T(8,128)(2,1)S(1)}, u32[]{:S(2)}, u32[]{:S(2)}) collective-permute-start(bf16[3,8,16,128]{3,2,1,0:T(8,128)(2,1)S(1)} %get-tuple-element.598), channel_id=1, source_target_pairs={{0,8},{2,10},{4,12},{6,14},{8,0},{10,2},{12,4},{14,6},{1,9},{3,11}... | collective-permute-start | bytes 294920 | tf_op jit(solution)/shard_map/cond/branch_55_fun/ppermute | solution.py:602
  31.5 7.6 %collective-permute-done.127 = bf16[3,8,16,128]{3,2,1,0:T(8,128)(2,1)S(1)} collective-permute-done((bf16[3,8,16,128]{3,2,1,0:T(8,128)(2,1)S(1)}, bf16[3,8,16,128]{3,2,1,0:T(8,128)(2,1)S(1)}, u32[]{:S(2)}, u32[]{:S(2)}) %collective-permute-start.127) | collective-permute-done | bytes 98336 | tf_op jit(solution)/shard_map/cond/branch_55_fun/ppermute | solution.py:602
  39.1 2.1 %collective-permute-done.128 = bf16[3,8,16,128]{3,2,1,0:T(8,128)(2,1)S(1)} collective-permute-done((bf16[3,8,16,128]{3,2,1,0:T(8,128)(2,1)S(1)}, bf16[3,8,16,128]{3,2,1,0:T(8,128)(2,1)S(1)}, u32[]{:S(2)}, u32[]{:S(2)}) %collective-permute-start.128) | collective-permute-done | bytes 98336 | tf_op jit(solution)/shard_map/cond/branch_55_fun/ppermute | solution.py:602
  41.2 2.5 %collective-permute-done.129 = bf16[3,8,16,128]{3,2,1,0:T(8,128)(2,1)S(1)} collective-permute-done((bf16[3,8,16,128]{3,2,1,0:T(8,128)(2,1)S(1)}, bf16[3,8,16,128]{3,2,1,0:T(8,128)(2,1)S(1)}, u32[]{:S(2)}, u32[]{:S(2)}) %collective-permute-start.129) | collective-permute-done | bytes 98336 | tf_op jit(solution)/shard_map/cond/branch_55_fun/ppermute | solution.py:602
  43.8 0.7 %collective-permute-start.174 = (bf16[3,8,16,128]{3,2,1,0:T(8,128)(2,1)S(1)}, bf16[3,8,16,128]{3,2,1,0:T(8,128)(2,1)S(1)}, u32[]{:S(2)}, u32[]{:S(2)}) collective-permute-start(bf16[3,8,16,128]{3,2,1,0:T(8,128)(2,1)S(1)} %get-tuple-element.662), channel_id=1, source_target_pairs={{0,8},{2,10},{4,12},{6,14},{8,0},{10,2},{12,4},{14,6},{1,9},{3,11}... | collective-permute-start | bytes 294920 | tf_op jit(solution)/shard_map/ppermute | solution.py:602
  44.5 2.3 %collective-permute-start.175 = (bf16[3,8,16,128]{3,2,1,0:T(8,128)(2,1)S(1)}, bf16[3,8,16,128]{3,2,1,0:T(8,128)(2,1)S(1)}, u32[]{:S(2)}, u32[]{:S(2)}) collective-permute-start(bf16[3,8,16,128]{3,2,1,0:T(8,128)(2,1)S(1)} %get-tuple-element.663), channel_id=1, source_target_pairs={{0,10},{2,12},{4,14},{6,0},{8,2},{10,4},{12,6},{14,8},{1,11},{3,13... | collective-permute-start | bytes 294920 | tf_op jit(solution)/shard_map/ppermute | solution.py:602
  46.8 0.7 %collective-permute-start.176 = (bf16[3,8,16,128]{3,2,1,0:T(8,128)(2,1)S(1)}, bf16[3,8,16,128]{3,2,1,0:T(8,128)(2,1)S(1)}, u32[]{:S(2)}, u32[]{:S(2)}) collective-permute-start(bf16[3,8,16,128]{3,2,1,0:T(8,128)(2,1)S(1)} %get-tuple-element.664), channel_id=1, source_target_pairs={{0,12},{2,14},{4,0},{6,2},{8,4},{10,6},{12,8},{14,10},{1,13},{3,15... | collective-permute-start | bytes 294920 | tf_op jit(solution)/shard_map/ppermute | solution.py:602
  47.5 5.9 %collective-permute-done.173.refs_2_ = bf16[3,8,16,128]{3,2,1,0:T(8,128)(2,1)S(1)} collective-permute-done((bf16[3,8,16,128]{3,2,1,0:T(8,128)(2,1)S(1)}, bf16[3,8,16,128]{3,2,1,0:T(8,128)(2,1)S(1)}, u32[]{:S(2)}, u32[]{:S(2)}) %collective-permute-start.173) | collective-permute-done | bytes 98336 | tf_op jit(solution)/shard_map/ppermute | solution.py:602
  53.4 2.2 %collective-permute-done.174.refs_3_ = bf16[3,8,16,128]{3,2,1,0:T(8,128)(2,1)S(1)} collective-permute-done((bf16[3,8,16,128]{3,2,1,0:T(8,128)(2,1)S(1)}, bf16[3,8,16,128]{3,2,1,0:T(8,128)(2,1)S(1)}, u32[]{:S(2)}, u32[]{:S(2)}) %collective-permute-start.174) | collective-permute-done | bytes 98336 | tf_op jit(solution)/shard_map/ppermute | solution.py:602
  56.1 5.8 %collective-permute-done.177.refs_6_ = bf16[3,8,16,128]{3,2,1,0:T(8,128)(2,1)S(1)} collective-permute-done((bf16[3,8,16,128]{3,2,1,0:T(8,128)(2,1)S(1)}, bf16[3,8,16,128]{3,2,1,0:T(8,128)(2,1)S(1)}, u32[]{:S(2)}, u32[]{:S(2)}) %collective-permute-start.177) | collective-permute-done | bytes 98336 | tf_op jit(solution)/shard_map/ppermute | solution.py:602
  61.8 1.4 %unpack.1 = bf16[22,8,16,128]{3,2,1,0:T(8,128)(2,1)} custom-call(s32[65]{0:T(128)S(1)} %copy-done.1, bf16[11,8,16,128]{3,2,1,0:T(8,128)(2,1)S(1)} %get-tuple-element.656.keep, bf16[11,8,16,128]{3,2,1,0:T(8,128)(2,1)S(1)} %collective-permute-done.170.other, bf16[3,8,16,128]{3,2,1,0:T(8,128)(2,1)S(1)} %collective-permute-done.171.refs_0_, ...), custom_call_target="tpu_custom_call" | custom-call | tf_op jit(solution)/shard_map/unpack/pallas_call | solution.py:628
  (40 shorter events, 1.1 us)
Async XLA Ops:
  0.0 6.2 %collective-permute-start.169 = (bf16[22,8,16,128]{3,2,1,0:T(8,128)(2,1)}, bf16[22,8,16,128]{3,2,1,0:T(8,128)(2,1)S(1)}, u32[]{:S(2)}, u32[]{:S(2)}) collective-permute-start(bf16[22,8,16,128]{3,2,1,0:T(8,128)(2,1)} %pair.1), channel_id=1, source_target_pairs={{0,1},{1,0},{2,3},{3,2},{4,5},{5,4},{6,7},{7,6},{8,9},{9,8},{10,11... | collective-permute-start | bytes 2162696 | tf_op jit(solution)/shard_map/ppermute | solution.py:670
  0.7 3.9 %copy-start.12 = (bf16[1024,128]{1,0:T(8,128)(2,1)S(1)}, bf16[1024,128]{1,0:T(8,128)(2,1)}, u32[]{:S(2)}) copy-start(bf16[1024,128]{1,0:T(8,128)(2,1)} %param.103) | copy-start | bytes 786436
  0.7 5.6 %copy-start.2 = (bf16[22,8,16,128]{3,2,1,0:T(8,128)(2,1)S(1)}, bf16[22,8,16,128]{3,2,1,0:T(8,128)(2,1)}, u32[]{:S(2)}) copy-start(bf16[22,8,16,128]{3,2,1,0:T(8,128)(2,1)} %pair.1) | copy-start | bytes 2162692
  0.7 5.6 %copy-start.3 = (bf16[128,512]{1,0:T(8,128)(2,1)S(1)}, bf16[128,512]{1,0:T(8,128)(2,1)}, u32[]{:S(2)}) copy-start(bf16[128,512]{1,0:T(8,128)(2,1)} %out_ab.1) | copy-start | bytes 393220
  0.7 5.6 %copy-start.5 = (bf16[128,128]{1,0:T(8,128)(2,1)S(1)}, bf16[128,128]{1,0:T(8,128)(2,1)}, u32[]{:S(2)}) copy-start(bf16[128,128]{1,0:T(8,128)(2,1)} %out_gate.1) | copy-start | bytes 98308
  0.7 5.6 %copy-start.6 = (bf16[128,128]{1,0:T(8,128)(2,1)S(1)}, bf16[128,128]{1,0:T(8,128)(2,1)}, u32[]{:S(2)}) copy-start(bf16[128,128]{1,0:T(8,128)(2,1)} %out_proj.1) | copy-start | bytes 98308
  0.7 5.6 %copy-start.7 = (bf16[128,128]{1,0:T(8,128)(2,1)S(1)}, bf16[128,128]{1,0:T(8,128)(2,1)}, u32[]{:S(2)}) copy-start(bf16[128,128]{1,0:T(8,128)(2,1)} %in_gate.1) | copy-start | bytes 98308
  0.7 5.6 %copy-start.8 = (bf16[128,128]{1,0:T(8,128)(2,1)S(1)}, bf16[128,128]{1,0:T(8,128)(2,1)}, u32[]{:S(2)}) copy-start(bf16[128,128]{1,0:T(8,128)(2,1)} %in_proj.1) | copy-start | bytes 98308
  0.7 5.6 %copy-start.9 = (s32[176]{0:T(256)S(1)}, s32[176]{0:T(256)}, u32[]{:S(2)}) copy-start(s32[176]{0:T(256)} %lengths_ref.1) | copy-start | bytes 2116
  0.7 5.6 %copy-start.10 = (s32[176]{0:T(256)S(1)}, s32[176]{0:T(256)}, u32[]{:S(2)}) copy-start(s32[176]{0:T(256)} %breaks_ref.1) | copy-start | bytes 2116
  0.7 5.6 %copy-start.11 = (bf16[2,128]{1,0:T(2,128)(2,1)S(1)}, bf16[2,128]{1,0:T(2,128)(2,1)}, u32[]{:S(2)}) copy-start(bf16[2,128]{1,0:T(2,128)(2,1)} %bias.1) | copy-start | bytes 1540
  4.5 1.7 %collective-permute-start.168 = (bf16[11,32,256]{2,1,0:T(8,128)(2,1)}, bf16[11,32,256]{2,1,0:T(8,128)(2,1)S(1)}, u32[]{:S(2)}, u32[]{:S(2)}) collective-permute-start(bf16[11,32,256]{2,1,0:T(8,128)(2,1)} %get-tuple-element.655), channel_id=1, source_target_pairs={{0,1},{1,0},{2,3},{3,2},{4,5},{5,4},{6,7},{7,6},{8,9},{9,8},{10,11... | collective-permute-start | bytes 540680 | tf_op jit(solution)/shard_map/ppermute | solution.py:673
  19.9 3.9 %collective-permute-start.170 = (bf16[11,8,16,128]{3,2,1,0:T(8,128)(2,1)S(1)}, bf16[11,8,16,128]{3,2,1,0:T(8,128)(2,1)S(1)}, u32[]{:S(2)}, u32[]{:S(2)}) collective-permute-start(bf16[11,8,16,128]{3,2,1,0:T(8,128)(2,1)S(1)} %get-tuple-element.657), channel_id=1, source_target_pairs={{0,1},{1,0},{2,3},{3,2},{4,5},{5,4},{6,7},{7,6},{8,9},{9,8},{10,11... | collective-permute-start | bytes 1081352 | tf_op jit(solution)/shard_map/ppermute | solution.py:680
  25.5 21.3 %collective-permute-start.171 = (bf16[3,8,16,128]{3,2,1,0:T(8,128)(2,1)S(1)}, bf16[3,8,16,128]{3,2,1,0:T(8,128)(2,1)S(1)}, u32[]{:S(2)}, u32[]{:S(2)}) collective-permute-start(bf16[3,8,16,128]{3,2,1,0:T(8,128)(2,1)S(1)} %get-tuple-element.659), channel_id=1, source_target_pairs={{0,2},{2,4},{4,6},{6,8},{8,10},{10,12},{12,14},{14,0},{1,3},{3,5},... | collective-permute-start | bytes 294920 | tf_op jit(solution)/shard_map/ppermute | solution.py:602
  26.8 20.8 %collective-permute-start.172 = (bf16[3,8,16,128]{3,2,1,0:T(8,128)(2,1)S(1)}, bf16[3,8,16,128]{3,2,1,0:T(8,128)(2,1)S(1)}, u32[]{:S(2)}, u32[]{:S(2)}) collective-permute-start(bf16[3,8,16,128]{3,2,1,0:T(8,128)(2,1)S(1)} %get-tuple-element.660), channel_id=1, source_target_pairs={{0,4},{2,6},{4,8},{6,10},{8,12},{10,14},{12,0},{14,2},{1,5},{3,7},... | collective-permute-start | bytes 294920 | tf_op jit(solution)/shard_map/ppermute | solution.py:602
  29.0 10.1 %collective-permute-start.127 = (bf16[3,8,16,128]{3,2,1,0:T(8,128)(2,1)S(1)}, bf16[3,8,16,128]{3,2,1,0:T(8,128)(2,1)S(1)}, u32[]{:S(2)}, u32[]{:S(2)}) collective-permute-start(bf16[3,8,16,128]{3,2,1,0:T(8,128)(2,1)S(1)} %get-tuple-element.597), channel_id=1, source_target_pairs={{0,6},{2,8},{4,10},{6,12},{8,14},{10,0},{12,2},{14,4},{1,7},{3,9},... | collective-permute-start | bytes 294920 | tf_op jit(solution)/shard_map/cond/branch_55_fun/ppermute | solution.py:602
  30.0 11.2 %collective-permute-start.128 = (bf16[3,8,16,128]{3,2,1,0:T(8,128)(2,1)S(1)}, bf16[3,8,16,128]{3,2,1,0:T(8,128)(2,1)S(1)}, u32[]{:S(2)}, u32[]{:S(2)}) collective-permute-start(bf16[3,8,16,128]{3,2,1,0:T(8,128)(2,1)S(1)} %get-tuple-element.598), channel_id=1, source_target_pairs={{0,8},{2,10},{4,12},{6,14},{8,0},{10,2},{12,4},{14,6},{1,9},{3,11}... | collective-permute-start | bytes 294920 | tf_op jit(solution)/shard_map/cond/branch_55_fun/ppermute | solution.py:602
  31.4 12.4 %collective-permute-start.129 = (bf16[3,8,16,128]{3,2,1,0:T(8,128)(2,1)S(1)}, bf16[3,8,16,128]{3,2,1,0:T(8,128)(2,1)S(1)}, u32[]{:S(2)}, u32[]{:S(2)}) collective-permute-start(bf16[3,8,16,128]{3,2,1,0:T(8,128)(2,1)S(1)} %get-tuple-element.599), channel_id=1, source_target_pairs={{0,12},{2,14},{4,0},{6,2},{8,4},{10,6},{12,8},{14,10},{1,13},{3,15... | collective-permute-start | bytes 294920 | tf_op jit(solution)/shard_map/cond/branch_55_fun/ppermute | solution.py:602
  43.7 18.1 %copy-start.1 = (s32[65]{0:T(128)S(1)}, s32[65]{0:T(128)}, u32[]{:S(2)}) copy-start(s32[65]{0:T(128)} %plan.1.plan_ref) | copy-start | bytes 784
  43.8 9.7 %collective-permute-start.173 = (bf16[3,8,16,128]{3,2,1,0:T(8,128)(2,1)S(1)}, bf16[3,8,16,128]{3,2,1,0:T(8,128)(2,1)S(1)}, u32[]{:S(2)}, u32[]{:S(2)}) collective-permute-start(bf16[3,8,16,128]{3,2,1,0:T(8,128)(2,1)S(1)} %get-tuple-element.661), channel_id=1, source_target_pairs={{0,6},{2,8},{4,10},{6,12},{8,14},{10,0},{12,2},{14,4},{1,7},{3,9},... | collective-permute-start | bytes 294920 | tf_op jit(solution)/shard_map/ppermute | solution.py:602
  43.8 11.9 %collective-permute-start.174 = (bf16[3,8,16,128]{3,2,1,0:T(8,128)(2,1)S(1)}, bf16[3,8,16,128]{3,2,1,0:T(8,128)(2,1)S(1)}, u32[]{:S(2)}, u32[]{:S(2)}) collective-permute-start(bf16[3,8,16,128]{3,2,1,0:T(8,128)(2,1)S(1)} %get-tuple-element.662), channel_id=1, source_target_pairs={{0,8},{2,10},{4,12},{6,14},{8,0},{10,2},{12,4},{14,6},{1,9},{3,11}... | collective-permute-start | bytes 294920 | tf_op jit(solution)/shard_map/ppermute | solution.py:602
  44.5 11.2 %collective-permute-start.175 = (bf16[3,8,16,128]{3,2,1,0:T(8,128)(2,1)S(1)}, bf16[3,8,16,128]{3,2,1,0:T(8,128)(2,1)S(1)}, u32[]{:S(2)}, u32[]{:S(2)}) collective-permute-start(bf16[3,8,16,128]{3,2,1,0:T(8,128)(2,1)S(1)} %get-tuple-element.663), channel_id=1, source_target_pairs={{0,10},{2,12},{4,14},{6,0},{8,2},{10,4},{12,6},{14,8},{1,11},{3,13... | collective-permute-start | bytes 294920 | tf_op jit(solution)/shard_map/ppermute | solution.py:602
  46.8 9.3 %collective-permute-start.176 = (bf16[3,8,16,128]{3,2,1,0:T(8,128)(2,1)S(1)}, bf16[3,8,16,128]{3,2,1,0:T(8,128)(2,1)S(1)}, u32[]{:S(2)}, u32[]{:S(2)}) collective-permute-start(bf16[3,8,16,128]{3,2,1,0:T(8,128)(2,1)S(1)} %get-tuple-element.664), channel_id=1, source_target_pairs={{0,12},{2,14},{4,0},{6,2},{8,4},{10,6},{12,8},{14,10},{1,13},{3,15... | collective-permute-start | bytes 294920 | tf_op jit(solution)/shard_map/ppermute | solution.py:602
  47.5 14.3 %collective-permute-start.177 = (bf16[3,8,16,128]{3,2,1,0:T(8,128)(2,1)S(1)}, bf16[3,8,16,128]{3,2,1,0:T(8,128)(2,1)S(1)}, u32[]{:S(2)}, u32[]{:S(2)}) collective-permute-start(bf16[3,8,16,128]{3,2,1,0:T(8,128)(2,1)S(1)} %get-tuple-element.665), channel_id=1, source_target_pairs={{0,14},{2,0},{4,2},{6,4},{8,6},{10,8},{12,10},{14,12},{1,15},{3,1}... | collective-permute-start | bytes 294920 | tf_op jit(solution)/shard_map/ppermute | solution.py:602
  (2 other events, 1.6 us)
